TPU v7x, 128 devices: a whole 4x4x4 slice. The times are simulated.
128 devices in a mesh: bin: 4 (over y), grp: 32 (over x, z, core).
Axes of the slice: x: 4, y: 4, z: 4, core: 2. Of those that a mesh axis runs over, the one named last changes fastest.
Arguments:
- templates: bfloat16 [131072, 512], P(('bin', 'grp')), may hold values from -6 to 6
- owner_device: int32 [131072, 1], P(('bin', 'grp')), may hold values from 0 to 127; in each aligned block of 1024 rows (0 to 1023, 1024 to 2047, ...) at most 16 rows name the same one
- rate_code: int32 [131072], P(('bin', 'grp')), may hold values from 0 to 4
- rate_gains: float32 [5, 512], replicated, may hold values from 0.5 to 2
- sketch: float32 [512, 256], replicated, may hold values from -6 to 6
- strain: float32 [2, 262144], P(None, 'grp'), may hold values from -6 to 6
Outputs:
- mixing: bfloat16 [131072, 256], P(('bin', 'grp'))
- spectrum: float32 [4, 256], P('bin')
- filtered_0: bfloat16 [4, 2, 262144, 256], P('bin', None, 'grp')
- filtered_1: bfloat16 [4, 2, 131072, 256], P('bin', None, 'grp')
- filtered_2: bfloat16 [4, 2, 65536, 256], P('bin', None, 'grp')
- filtered_3: bfloat16 [4, 2, 32768, 256], P('bin', None, 'grp')
- filtered_4: bfloat16 [4, 2, 16384, 256], P('bin', None, 'grp')
Inputs may be any that keep to these rules, and one draw needn't show every extreme that they name: `owner_device`: among the rows of one device, no device is named by more than 16 rows, and some device is named by exactly 16 rows.
All inputs are finite; a program needn't handle non-finite values.
Results may differ from a plain program's by a relative error of at most 0.0059.
Values may be sent and summed in bfloat16 or wider, within the bound.
A program may use at most 128 MiB of HBM per device.

v0:
```python
import math

import jax
import jax.numpy as jnp
from jax import lax
from jax.sharding import PartitionSpec as P

highest = lax.Precision.HIGHEST
inv_root_two = 0.7071067811865476


def shifted(x, axis, by):
    length = lax.axis_size(axis)
    pairs = [(i, i + by) for i in range(length) if 0 <= i + by < length]
    return lax.ppermute(x, axis, pairs)


def whiten_rows(templates, rate_code, rate_gains):
    factor = jnp.zeros(templates.shape, jnp.float32)
    for rate_level in range(rate_gains.shape[0]):
        factor = factor + jnp.where(
            (rate_code == rate_level)[:, None], rate_gains[rate_level][None, :], jnp.float32(0.0)
        )
    return (templates.astype(jnp.float32) * factor).astype(jnp.bfloat16)


def strain_levels(strain, count):
    current = strain
    level_list = []
    for rate_level in range(count):
        if rate_level > 0:
            paired = current.reshape(current.shape[0], -1, 2)
            current = (paired[:, :, 0] + paired[:, :, 1]) * inv_root_two
        level_list.append(current.astype(jnp.bfloat16))
    return level_list


def filter_level(history, rounded, basis_bf, stride):
    tap_rows = basis_bf[::stride]
    joined = jnp.concatenate([history[:, 1:], rounded], axis=1)
    return lax.conv_general_dilated(
        joined[:, :, None],
        tap_rows[::-1][:, None, :],
        (1,),
        "VALID",
        dimension_numbers=("NWC", "WIO", "NWC"),
        preferred_element_type=jnp.float32,
    )


def basis_from(product):
    inner_gram = jnp.dot(product.T, product, precision=highest)
    lower_factor = jnp.linalg.cholesky(inner_gram)
    basis_bf = jax.scipy.linalg.solve_triangular(lower_factor, product.T, lower=True).T.astype(
        jnp.bfloat16
    )
    return (basis_bf, jnp.diagonal(lower_factor))


def local(templates, owner_device, rate_code, rate_gains, sketch, strain):
    tpl_rows = templates.shape[0]
    slice_len = templates.shape[1]
    group_size = lax.axis_size("grp")
    bin_count = lax.axis_size("bin")
    devices = bin_count * group_size
    capacity = 2 * tpl_rows // devices
    scale_down = tpl_rows * group_size * math.sqrt(slice_len)
    whitened = whiten_rows(templates, rate_code, rate_gains)
    target = owner_device[:, 0]
    member_table = (target[:, None] == jnp.arange(devices, dtype=jnp.int32)[None, :]).astype(
        jnp.int32
    )
    rank_in_dest = jnp.sum(jnp.cumsum(member_table, axis=0) * member_table, axis=1) - 1
    slot_index = target * capacity + rank_in_dest
    outgoing = jnp.zeros((devices * capacity, slice_len), jnp.bfloat16).at[slot_index].set(whitened)
    received = lax.all_to_all(outgoing, ("bin", "grp"), split_axis=0, concat_axis=0, tiled=True)
    partial_gram = lax.dot_general(
        received, received, (((0,), (0,)), ((), ())), preferred_element_type=jnp.float32
    )
    gram_total = lax.psum(partial_gram, "grp")
    product = jnp.dot(gram_total, sketch, precision=highest)
    basis_bf, diag_here = basis_from(product)
    coeffs = jnp.dot(received, basis_bf, preferred_element_type=jnp.float32).astype(jnp.bfloat16)
    returned = lax.all_to_all(coeffs, ("bin", "grp"), split_axis=0, concat_axis=0, tiled=True)
    mixing = returned[slot_index]
    spectrum = (diag_here / scale_down)[None, :]
    levels = strain_levels(strain, rate_gains.shape[0])
    rim_list = [
        levels[rate_level][:, -(slice_len >> rate_level) :] for rate_level in range(len(levels))
    ]
    history = shifted((rim_list[0], rim_list[1], rim_list[2], rim_list[3], rim_list[4]), "grp", 1)
    filtered = []
    for rate_level in range(len(levels)):
        result_level = filter_level(
            history[rate_level], levels[rate_level], basis_bf, 2**rate_level
        )
        filtered.append(result_level.astype(jnp.bfloat16)[None])
    return (mixing, spectrum, filtered[0], filtered[1], filtered[2], filtered[3], filtered[4])


def solution(mesh):
    return jax.shard_map(
        local,
        mesh=mesh,
        in_specs=(
            P(("bin", "grp"), None),
            P(("bin", "grp"), None),
            P(("bin", "grp")),
            P(),
            P(),
            P(None, "grp"),
        ),
        out_specs=(
            P(("bin", "grp"), None),
            P("bin", None),
            P("bin", None, "grp", None),
            P("bin", None, "grp", None),
            P("bin", None, "grp", None),
            P("bin", None, "grp", None),
            P("bin", None, "grp", None),
        ),
        check_vma=False,
    )
```

profile of v0, /device:TPU:1, one launch (start us, length us, event | category | flops | bytes accessed | tf_op | source)
XLA Modules:
  0.0 488.3 jit_solution(5350892277837483940)
XLA Ops:
  7.2 0.9 copy.22
  9.0 7.3 %scatter_custom_fusion = bf16[2048,512]{1,0:T(8,128)(2,1)} fusion(s32[1024]{0:T(1024)S(1)} %bitcast.143, bf16[1024,512]{1,0:T(8,128)(2,1)S(1)} %copy-done.3, f32[512]{0:T(512)S(1)} %bitcast.149, f32[512]{0:T(512)S(1)} %bitcast.150, f32[512]{0:T(512)S(1)} %bitcast.147, f32[512]{0:T(512)S(1)} %bitcast.148, f32[]{:T(128)} %constant.105.clone.1, ...), kind=kCustom, calls=%fused_computation.26 | custom fusion | flops 6291456 | bytes 3161094 | tf_op jit(solution)/shard_map/scatter | solution.py:75
  16.3 12.0 %all-to-all-start = ((bf16[128,16,512]{2,1,0:T(8,128)(2,1)}), bf16[128,16,512]{2,1,0:T(8,128)(2,1)}, u32[]{:S(2)}, u32[]{:S(2)}) async-start(bf16[128,16,512]{2,1,0:T(8,128)(2,1)} %bitcast.12), calls=%async_computation | async-start | bytes 4194304 | tf_op jit(solution)/shard_map/all_to_all | solution.py:76
  28.4 3.7 collective-permute-start
  32.1 6.4 %reshape.114 = f32[2,4096,2]{2,1,0:T(8,128)} reshape(f32[2,8192]{1,0:T(2,128)S(1)} %copy-done.6) | data formatting | bytes 131072 | tf_op jit(solution)/shard_map/reshape | solution.py:32
  38.5 5.9 %convert_reduce_fusion = bf16[2,4096]{1,0:T(2,128)(2,1)S(1)} fusion(f32[2,4096,2]{2,1,0:T(8,128)} %reshape.114), kind=kLoop, calls=%fused_computation.17 | loop fusion | flops 24576 | bytes 81920 | tf_op jit(solution)/shard_map/convert_element_type | solution.py:34
  44.4 2.5 collective-permute-start.1
  46.9 2.4 fusion.3
  49.3 2.2 mul.59
  51.5 1.2 convert_reduce_fusion.1
  52.7 3.6 collective-permute-start.2
  56.3 1.2 fusion.18
  57.5 1.0 mul.62
  59.3 2.1 collective-permute-start.3
  63.0 3.3 collective-permute-start.4
  69.6 0.8 copy.31
  70.8 1.1 copy.28
  72.0 4.5 convolution_bitcast_fusion
  76.8 1.4 copy.25
  78.2 104.7 %all-reduce.3.cloned.1.call-done = f32[512,512]{1,0:T(8,128)} async-done(((f32[512,512]{1,0:T(8,128)}), f32[512,512]{1,0:T(8,128)}) %all-reduce.3.cloned.1.call-update) | async-done | bytes 1048592 | tf_op jit(solution)/shard_map/psum | solution.py:80
  183.0 2.2 fusion.55
  185.2 1.0 fusion.56
  186.5 11.7 %cholesky.50 = f32[128,128]{1,0:T(8,128)S(1)} custom-call(f32[128,128]{1,0:T(8,128)S(1)} %cholesky.118), custom_call_target="Cholesky" | custom-call | tf_op jit(solution)/shard_map/jit(cholesky)/cholesky | solution.py:53
  198.2 9.8 %custom-call.15 = f32[1,128,128]{1,2,0:T(8,128)S(1)} custom-call(f32[1,128,128]{2,1,0:T(8,128)S(1)} %get-tuple-element.30), custom_call_target="InvertDiagBlocksLowerTriangular" | custom-call | tf_op jit(solution)/shard_map/jit(cholesky)/cholesky | solution.py:53
  208.5 12.1 %cholesky.105 = f32[128,128]{1,0:T(8,128)S(1)} custom-call(f32[128,128]{1,0:T(8,128)S(1)} %convolution_subtract_fusion.1), custom_call_target="Cholesky" | custom-call | tf_op jit(solution)/shard_map/jit(cholesky)/cholesky | solution.py:53
  222.7 4.0 while.1
  223.3 1.4 bitcast_dynamic-update-slice_fusion.2
  225.3 1.4 bitcast_dynamic-update-slice_fusion.2
  226.7 19.7 %custom-call.16 = f32[2,128,128]{1,2,0:T(8,128)S(1)} custom-call(f32[2,128,128]{2,1,0:T(8,128)S(1)} %get-tuple-element.14), custom_call_target="InvertDiagBlocksLowerTriangular" | custom-call | tf_op jit(solution)/shard_map/jit(_solve_triangular)/triangular_solve | solution.py:54
  247.9 0.8 rev.15
  248.8 6.6 %slice.147 = bf16[256,256]{0,1:T(8,128)(2,1)} slice(bf16[512,256]{0,1:T(8,128)(2,1)S(1)} %fusion.31), slice={[0:512:2], [0:256:1]} | slice | bytes 262144 | tf_op jit(solution)/shard_map/slice | solution.py:39
  255.4 3.0 slice.152
  258.3 1.9 slice.157
  260.2 1.3 slice.162
  261.5 3.3 convolution_convert_fusion
  264.9 8.5 %all-to-all-start.1 = ((bf16[128,16,256]{2,1,0:T(8,128)(2,1)}), bf16[128,16,256]{2,1,0:T(8,128)(2,1)}, u32[]{:S(2)}, u32[]{:S(2)}) async-start(bf16[128,16,256]{2,1,0:T(8,128)(2,1)} %bitcast.21), calls=%async_computation.1 | async-start | bytes 2097152 | tf_op jit(solution)/shard_map/all_to_all | solution.py:84
  273.3 2.3 gather_fusion.1
  276.7 123.6 %select_convert_fusion = bf16[16,1088,256]{2,0,1:T(8,128)(2,1)} fusion(pred[16,1088]{0,1:T(8,128)(4,1)S(1)} %bitcast.152, bf16[16,1599,1]{0,2,1:T(2,128)(2,1)S(1)} %copy.25, bf16[512,1,256]{2,1,0:T(2,128)(2,1)S(1)} %copy.26), kind=kOutput, calls=%fused_computation.5 | convolution fusion | flops 4572315648 | bytes 9243616 | tf_op jit(solution)/shard_map/conv_general_dilated | solution.py:41
  400.3 10.2 %copy.27 = bf16[16,1088,256]{2,1,0:T(8,128)(2,1)} copy(bf16[16,1088,256]{2,0,1:T(8,128)(2,1)} %select_convert_fusion) | data formatting | bytes 17825792 | tf_op jit(solution)/shard_map/convert_element_type | solution.py:97
  410.5 7.4 %slice_bitcast_fusion = bf16[1,2,8192,256]{3,2,1,0:T(8,128)(2,1)} fusion(bf16[2,8704,256]{2,1,0:T(8,128)(2,1)} %bitcast.129), kind=kLoop, calls=%fused_computation.7 | loop fusion | bytes 16777216 | tf_op jit(solution)/shard_map/broadcast_in_dim | solution.py:97
  418.6 31.3 %select_convert_fusion.1 = bf16[16,544,256]{2,0,1:T(8,128)(2,1)S(1)} fusion(pred[16,544]{0,1:T(8,128)(4,1)S(1)} %bitcast.153, bf16[16,799,1]{0,2,1:T(2,128)(2,1)S(1)} %copy-done.5, bf16[256,1,256]{2,1,0:T(2,128)(2,1)S(1)} %copy.29), kind=kOutput, calls=%fused_computation.6 | convolution fusion | flops 1145307136 | bytes 4621792 | tf_op jit(solution)/shard_map/conv_general_dilated | solution.py:41
  449.9 3.6 copy.30
  453.8 8.4 %select_convert_fusion.2 = bf16[16,272,256]{2,0,1:T(8,128)(2,1)S(1)} fusion(pred[16,272]{0,1:T(8,128)(4,1)S(1)} %copy-done.19, bf16[16,399,1]{0,2,1:T(2,128)(2,1)S(1)} %copy-done.10, bf16[128,1,256]{2,1,0:T(2,128)(2,1)S(1)} %copy.32), kind=kOutput, calls=%fused_computation.8 | convolution fusion | flops 287440896 | bytes 2310880 | tf_op jit(solution)/shard_map/conv_general_dilated | solution.py:41
  463.0 1.5 slice_bitcast_fusion.2
  464.8 2.5 select_convert_fusion.3
  467.7 1.0 slice_bitcast_fusion.3
  470.8 4.5 slice_bitcast_fusion.1
  475.3 6.0 %gather_fusion = bf16[1024,256]{1,0:T(8,128)(2,1)} fusion(bf16[2048,256]{1,0:T(8,128)(2,1)} %bitcast.22, s32[1024]{0:T(1024)S(1)} %copy-done.14), kind=kCustom, calls=%fused_computation | custom fusion | bytes 1052672 | tf_op jit(solution)/shard_map/gather | solution.py:85
  (145 shorter events, 16.9 us)
Async XLA Ops:
  7.2 175.8 %copy-start = (f32[512,256]{1,0:T(8,128)S(1)}, f32[512,256]{1,0:T(8,128)}, u32[]{:S(2)}) copy-start(f32[512,256]{1,0:T(8,128)} %param.10) | copy-start | bytes 1572868
  7.2 1.3 copy-start.13
  7.2 1.7 copy-start.15
  7.2 1.8 copy-start.16
  7.2 1.8 copy-start.3
  16.3 12.0 %copy-start.6 = (f32[2,8192]{1,0:T(2,128)S(1)}, f32[2,8192]{1,0:T(2,128)}, u32[]{:S(2)}) copy-start(f32[2,8192]{1,0:T(2,128)} %param.11) | copy-start | bytes 196612
  16.3 55.6 %all-to-all-start = ((bf16[128,16,512]{2,1,0:T(8,128)(2,1)}), bf16[128,16,512]{2,1,0:T(8,128)(2,1)}, u32[]{:S(2)}, u32[]{:S(2)}) async-start(bf16[128,16,512]{2,1,0:T(8,128)(2,1)} %bitcast.12), calls=%async_computation | async-start | bytes 4194304 | tf_op jit(solution)/shard_map/all_to_all | solution.py:76
  28.3 154.7 %all-reduce.3.cloned.1.call-start = ((), (), s32[]{:S(2)}) async-start(), calls=%async_computation.2 | async-start | bytes 2097152 | tf_op jit(solution)/shard_map/psum | solution.py:80
  28.4 43.5 %collective-permute-start = (bf16[2,512]{1,0:T(2,128)(2,1)S(1)}, bf16[2,512]{1,0:T(2,128)(2,1)S(1)}, u32[]{:S(2)}, u32[]{:S(2)}) collective-permute-start(bf16[2,512]{1,0:T(2,128)(2,1)S(1)} %slice.190), channel_id=1, source_target_pairs={{0,1},{1,2},{2,3},{3,4},{4,5},{5,6},{6,7},{7,8},{8,9},{9,10},{10,1... | collective-permute-start | bytes 6152 | tf_op jit(solution)/shard_map/ppermute | solution.py:15
  38.5 8.4 %copy-start.2 = (f32[2,4096,2]{2,1,0:T(8,128)S(1)}, f32[2,4096,2]{2,1,0:T(8,128)}, u32[]{:S(2)}) copy-start(f32[2,4096,2]{2,1,0:T(8,128)} %reshape.114) | copy-start | bytes 196612
  44.4 26.0 %collective-permute-start.1 = (bf16[2,256]{1,0:T(2,128)(2,1)S(1)}, bf16[2,256]{1,0:T(2,128)(2,1)S(1)}, u32[]{:S(2)}, u32[]{:S(2)}) collective-permute-start(bf16[2,256]{1,0:T(2,128)(2,1)S(1)} %slice.196), channel_id=1, source_target_pairs={{0,1},{1,2},{2,3},{3,4},{4,5},{5,6},{6,7},{7,8},{8,9},{9,10},{10,1... | collective-permute-start | bytes 3080 | tf_op jit(solution)/shard_map/ppermute | solution.py:15
  52.7 16.5 %collective-permute-start.2 = (bf16[2,128]{1,0:T(2,128)(2,1)S(1)}, bf16[2,128]{1,0:T(2,128)(2,1)S(1)}, u32[]{:S(2)}, u32[]{:S(2)}) collective-permute-start(bf16[2,128]{1,0:T(2,128)(2,1)S(1)} %slice.202), channel_id=1, source_target_pairs={{0,1},{1,2},{2,3},{3,4},{4,5},{5,6},{6,7},{7,8},{8,9},{9,10},{10,1... | collective-permute-start | bytes 1544 | tf_op jit(solution)/shard_map/ppermute | solution.py:15
  59.3 8.8 %collective-permute-start.3 = (bf16[2,64]{1,0:T(2,128)(2,1)S(1)}, bf16[2,64]{1,0:T(2,128)(2,1)S(1)}, u32[]{:S(2)}, u32[]{:S(2)}) collective-permute-start(bf16[2,64]{1,0:T(2,128)(2,1)S(1)} %slice.207), channel_id=1, source_target_pairs={{0,1},{1,2},{2,3},{3,4},{4,5},{5,6},{6,7},{7,8},{8,9},{9,10},{10,1... | collective-permute-start | bytes 776 | tf_op jit(solution)/shard_map/ppermute | solution.py:15
  63.0 4.0 collective-permute-start.4
  264.9 11.8 %copy-start.17 = (pred[16,1088]{0,1:T(32,128)(4,1)S(1)}, pred[16,1088]{0,1:T(32,128)(4,1)}, u32[]{:S(2)}) copy-start(pred[16,1088]{0,1:T(32,128)(4,1)} %constant.152) | copy-start | bytes 52228
  264.9 210.4 %all-to-all-start.1 = ((bf16[128,16,256]{2,1,0:T(8,128)(2,1)}), bf16[128,16,256]{2,1,0:T(8,128)(2,1)}, u32[]{:S(2)}, u32[]{:S(2)}) async-start(bf16[128,16,256]{2,1,0:T(8,128)(2,1)} %bitcast.21), calls=%async_computation.1 | async-start | bytes 2097152 | tf_op jit(solution)/shard_map/all_to_all | solution.py:84
  410.5 7.4 %copy-start.4 = (bf16[256,256]{0,1:T(8,128)(2,1)S(1)}, bf16[256,256]{0,1:T(8,128)(2,1)}, u32[]{:S(2)}) copy-start(bf16[256,256]{0,1:T(8,128)(2,1)} %slice.147) | copy-start | bytes 393220
  410.5 8.0 %copy-start.5 = (bf16[16,799,1]{0,2,1:T(2,128)(2,1)S(1)}, bf16[16,799,1]{0,2,1:T(2,128)(2,1)}, u32[]{:S(2)}) copy-start(bf16[16,799,1]{0,2,1:T(2,128)(2,1)} %copy.28) | copy-start | bytes 76708
  410.5 8.0 %copy-start.18 = (pred[16,544]{0,1:T(32,128)(4,1)S(1)}, pred[16,544]{0,1:T(32,128)(4,1)}, u32[]{:S(2)}) copy-start(pred[16,544]{0,1:T(32,128)(4,1)} %constant.153) | copy-start | bytes 26116
  449.8 3.7 copy-start.9
  449.8 4.0 copy-start.10
  449.8 4.0 copy-start.19
  463.0 1.5 copy-start.8
  463.0 1.8 copy-start.11
  463.0 1.8 copy-start.20
  467.3 1.4 copy-start.7
  467.3 1.7 copy-start.12
  467.3 1.7 copy-start.21
  470.8 4.5 copy-start.14
  475.3 6.0 %copy-start.1 = (f32[512,256]{1,0:T(8,128)S(1)}, f32[512,256]{1,0:T(8,128)}, u32[]{:S(2)}) copy-start(f32[512,256]{1,0:T(8,128)} %param.10) | copy-start | bytes 1572868
Sparse Core Ops, SparseCore 0:
  76.6 106.3 all-reduce.2
where the time goes:
time: 496 us; the launch traced here: 488 us
  matrix products  179 us (36%)
  waiting for transfers between devices  105 us (21%)
  other arithmetic  76.5 us (15%)
  local copies, waits for them, and re-layouts  75.7 us (15%)
  starting transfers between devices  35.6 us (7%)
  between operations  16.3 us (3%)
    conv_general_dilated x5, matrix products, filter_level(): lax.conv_general_dilated(joined[:, :, None], tap_rows[::-1][:, None, :],...  166 us
    psum x1, waiting for transfers between devices, local(): gram_total = lax.psum(partial_gram, 'grp')  105 us
    another operation x6, other arithmetic, basis_from(): lower_factor = jnp.linalg.cholesky(inner_gram)  34.3 us
    another operation x3, other arithmetic, basis_from(): jax.scipy.linalg.solve_triangular(lower_factor, product.T, lower=True)  19.7 us
    convert_element_type x6, local copies, waits for them, and re-layouts, local(): filtered.append(result_level.astype(jnp.bfloat16)[None])  15.2 us
    broadcast_in_dim x5, local copies, waits for them, and re-layouts, local(): filtered.append(result_level.astype(jnp.bfloat16)[None])  15.2 us
    ppermute x5, starting transfers between devices, shifted(): return lax.ppermute(x, axis, pairs)  15.1 us
    slice x4, local copies, waits for them, and re-layouts, filter_level(): tap_rows = basis_bf[::stride]  12.8 us
  transfers between devices with their start and end apart: 8, of which 2 were waited for; matrix products, arithmetic and copies ran while one was open for 47% of the time, Pallas kernels for 0%

commit v1 on v0

v1 whole, which is shorter than its diff:
```python
import functools
import math

import jax
import jax.numpy as jnp
from jax import lax
from jax.experimental import pallas as pl
from jax.experimental.pallas import tpu as pltpu
from jax.sharding import PartitionSpec as P

f32, bf16 = jnp.float32, jnp.bfloat16
highest = lax.Precision.HIGHEST
inv_root_two = 0.7071067811865476
LANES = 128
VMEM_LIMIT = 56 << 20


def dot(a, b, ca, cb, precision=None):
    return lax.dot_general(
        a, b, (((ca,), (cb,)), ((), ())), precision=precision, preferred_element_type=f32
    )


def split(x, parts):
    out = []
    for _ in range(parts):
        piece = x.astype(bf16)
        out.append(piece)
        x = x - piece.astype(f32)
    return out


def partial_kernel(bins, t_ref, code_ref, gains_ref, sketch_ref, white_ref, part_ref):
    rows, length = t_ref.shape
    width = sketch_ref.shape[1]
    code = code_ref[...]
    rate = jnp.broadcast_to(code % 8, (24, rows))
    which = lax.broadcasted_iota(jnp.int32, (24, rows), 0) % 8
    onehot = jnp.where(rate == which, 1.0, 0.0).astype(bf16)
    gains = gains_ref[...]
    gains = jnp.concatenate(split(gains, 3), axis=0)
    factor = dot(onehot, gains, 0, 0)
    white = (t_ref[...].astype(f32) * factor).astype(bf16)
    white_ref[...] = white
    sk = split(sketch_ref[...], 2)
    y = dot(white, sk[0], 1, 0) + dot(white, sk[1], 1, 0)
    bin_col = jnp.transpose(jnp.broadcast_to(code // 8, (8, rows)).astype(f32))[:, 0:1]
    yh, yl = split(y, 2)
    yh, yl = yh.astype(f32), yl.astype(f32)
    for b in range(bins):
        m = bin_col == float(b)
        yb = jnp.concatenate(
            [jnp.where(m, yh, 0.0).astype(bf16), jnp.where(m, yl, 0.0).astype(bf16)], axis=1
        )
        pb = dot(white, yb, 0, 0)
        part_ref[b] = pb[:, :width] + pb[:, width:]


def eliminate(D, nb, w=8):
    groups = nb // 8
    W2 = 2 * nb
    ri = lax.broadcasted_iota(jnp.int32, (nb, nb), 0)
    ci = lax.broadcasted_iota(jnp.int32, (nb, nb), 1)
    eye = jnp.where(ri == ci, 1.0, 0.0).astype(f32)
    M = jnp.concatenate([D, eye], axis=1)
    Mv = [M[8 * k : 8 * k + 8, :] for k in range(groups)]
    sub = lax.broadcasted_iota(jnp.int32, (8, W2), 0)
    spread = lambda x: jnp.broadcast_to(x, (8, W2))
    for j in range(0, nb, w):
        g = j // 8
        a = [spread(Mv[(j + s) // 8][(j + s) % 8 : (j + s) % 8 + 1, :]) for s in range(w)]
        S = [
            [spread(a[s][:, j + t : j + t + 1]) if t >= s else None for t in range(w)]
            for s in range(w)
        ]
        c = {k: [spread(Mv[k][:, j + s : j + s + 1]) for s in range(w)] for k in range(g, groups)}
        inv = []
        for s in range(w):
            iv = 1.0 / S[s][s]
            inv.append(iv)
            for t in range(s + 1, w):
                f = S[s][t] * iv
                for u in range(t, w):
                    S[t][u] = S[t][u] - f * S[s][u]
                a[t] = a[t] - f * a[s]
        for k in range(g, groups):
            acc = Mv[k]
            for s in range(w):
                m = c[k][s] * inv[s]
                if k * 8 <= j + s:
                    m = jnp.where(sub + 8 * k > j + s, m, 0.0)
                acc = acc - m * a[s]
                for t in range(s + 1, w):
                    c[k][t] = c[k][t] - m * S[s][t]
            Mv[k] = acc
    M = jnp.concatenate(Mv, axis=0)
    diag = jnp.where(ri == ci, M[:, :nb], 0.0)
    d_col = jnp.sum(diag, axis=1, keepdims=True)
    d_row = jnp.sum(diag, axis=0, keepdims=True)
    return M[:, nb:] * lax.rsqrt(d_col), d_row * lax.rsqrt(d_row)


def basis_steps(product, scale, A, X, spec_ref):
    n, nb = product.shape[1], 128
    A[...] = dot(product, product, 0, 0, highest)
    X0, d0 = eliminate(A[:nb, :nb], nb)
    R = dot(X0, A[:nb, nb:], 1, 0, highest)
    X1, d1 = eliminate(A[nb:, nb:] - dot(R, R, 0, 0, highest), nb)
    X[:nb, :nb] = X0
    X[:nb, nb:] = jnp.zeros((nb, n - nb), f32)
    X[nb:, nb:] = X1
    X[nb:, :nb] = -dot(X1, dot(R, X0, 0, 0, highest), 1, 0, highest)
    spec_ref[...] = jnp.concatenate([d0, d1], axis=1) * scale
    return dot(product, X[...], 1, 1, highest).astype(bf16)


def basis_kernel(scale, p_ref, basis_ref, spec_ref, A, X):
    basis_ref[...] = basis_steps(p_ref[...], scale, A, X, spec_ref)


def filter_kernel(lead, xe_ref, basis_ref, *rest):
    outs, (rv0, rv1, rv2, rv3, rv4, bwide, strip), (o0, o1, o2, o3, o4), sems = (
        rest[:5], rest[5:12], rest[12:17], rest[17]
    )
    rvs, obufs = (rv0, rv1, rv2, rv3, rv4), (o0, o1, o2, o3, o4)
    levels = len(outs)
    n = LANES
    ri = lax.broadcasted_iota(jnp.int32, (n, n), 0)
    ci = lax.broadcasted_iota(jnp.int32, (n, n), 1)
    flip = jnp.where(ri + ci == n - 1, 1.0, 0.0).astype(f32)
    first = jnp.where(ri // 2 == ci, 1.0, 0.0).astype(f32)
    second = jnp.where(ri // 2 == ci - n // 2, 1.0, 0.0).astype(f32)
    rv0[...] = dot(xe_ref[...], flip, 1, 0, highest)
    for r in range(1, levels):
        count = rvs[r].shape[0]
        later = rvs[r - 1][pl.ds(1, count, stride=2), :]
        earlier = rvs[r - 1][pl.ds(0, count, stride=2), :]
        rvs[r][...] = (
            dot(later, first, 1, 0, highest) + dot(earlier, second, 1, 0, highest)
        ) * inv_root_two
    for h in range(bwide.shape[0]):
        bwide[h] = basis_ref[:, h * n : (h + 1) * n].astype(f32)

    def every(taps, step):
        halves = [bwide[h, pl.ds(0, taps, stride=step), :] for h in range(bwide.shape[0])]
        return jnp.concatenate(halves, axis=1)

    length, width = basis_ref.shape
    base = 0
    copies = []
    for r in range(levels):
        taps = length >> r
        blocks = max(1, taps // n)
        rows = rvs[r].shape[0] // 2
        head = lead >> r
        tiles = rows - head
        held = tiles + blocks - 1
        if taps >= n:
            weight = every(taps, 1 << r).astype(bf16) if r else basis_ref[...]
        else:
            weight = jnp.concatenate(
                [every(taps, 1 << r), jnp.zeros((n - taps, width), f32)], axis=0
            ).astype(bf16)
        bwide_r = weight
        group = min(8, tiles)
        for d in range(2):
            first_col = base

            def build(p, carry, r=r, d=d, rows=rows, first_col=first_col):
                q = d * rows + rows - 1 - p
                z = jnp.concatenate(
                    [rvs[r][pl.ds(q, 1), :], rvs[r][pl.ds(q - 1, 1), :]], axis=1
                ).astype(bf16).astype(f32)
                z = jnp.broadcast_to(z, (n, 2 * n))
                t = pltpu.roll(z, n + 1, 1, stride=1, stride_axis=0)[:, :n]
                strip[:, pl.ds(pl.multiple_of((first_col + p) * n, n), n)] = t.astype(bf16)
                return carry

            lax.fori_loop(0, held, build, 0)

            def tile(s, carry, r=r, d=d, rows=rows, first_col=first_col, group=group,
                     blocks=blocks, weight=bwide_r, tiles=tiles):
                parts = []
                for i in range(group):
                    p = first_col + tiles - 1 - (s * group + i)
                    parts.append(strip[:, pl.ds(pl.multiple_of(p * n, n), blocks * n)])
                lhs = jnp.concatenate(parts, axis=0)
                span = group * n
                obufs[r][d, pl.ds(pl.multiple_of(s * span, span), span), :] = dot(
                    lhs, weight, 1, 0
                ).astype(bf16)
                pltpu.make_async_copy(
                    obufs[r].at[d, pl.ds(pl.multiple_of(s * span, span), span), :],
                    outs[r].at[0, d, pl.ds(pl.multiple_of(s * span, span), span), :],
                    sems.at[r],
                ).start()
                return carry

            lax.fori_loop(0, tiles // group, tile, 0)
            base += held
    for r in range(levels):
        pltpu.make_async_copy(obufs[r], outs[r].at[0], sems.at[r]).wait()


def filters(xe, basis, lead, levels):
    rows = xe.shape[0]
    length, width = basis.shape
    samples = (rows // 2 - lead) * LANES
    held = sum(
        2 * ((samples >> r) // LANES + max(1, (length >> r) // LANES) - 1) for r in range(levels)
    )
    vm = lambda: pl.BlockSpec(memory_space=pltpu.VMEM)
    return pl.pallas_call(
        functools.partial(filter_kernel, lead),
        out_shape=[
            jax.ShapeDtypeStruct((1, 2, samples >> r, width), bf16) for r in range(levels)
        ],
        in_specs=[vm(), vm()],
        out_specs=[pl.BlockSpec(memory_space=pl.ANY)] * levels,
        scratch_shapes=[pltpu.VMEM((rows >> r, LANES), f32) for r in range(levels)]
        + [pltpu.VMEM((width // LANES, length, LANES), f32), pltpu.VMEM((LANES, held * LANES), bf16)]
        + [pltpu.VMEM((2, samples >> r, width), bf16) for r in range(levels)]
        + [pltpu.SemaphoreType.DMA((levels,))],
        compiler_params=pltpu.CompilerParams(vmem_limit_bytes=VMEM_LIMIT),
        name="filters",
    )(xe, basis)


def mixing_kernel(bins, white_ref, code_ref, bases_ref, out_ref):
    rows = white_ref.shape[0]
    white = white_ref[...]
    bin_col = jnp.transpose(jnp.broadcast_to(code_ref[...] // 8, (8, rows)).astype(f32))[:, 0:1]
    acc = None
    for b in range(bins):
        mixed = dot(white, bases_ref[b], 1, 0)
        acc = mixed if acc is None else jnp.where(bin_col == float(b), mixed, acc)
    out_ref[...] = acc.astype(bf16)


def local(bins, group_size, templates, owner_device, rate_code, rate_gains, sketch, strain):
    rows, length = templates.shape
    width = sketch.shape[1]
    levels = rate_gains.shape[0]
    lead = 16
    scale = 1.0 / (rows * group_size * math.sqrt(length))
    params = pltpu.CompilerParams(vmem_limit_bytes=VMEM_LIMIT)
    code = (owner_device[:, 0] // group_size * 8 + rate_code)[None, :]
    gains = jnp.concatenate([rate_gains, jnp.zeros((8 - levels, length), f32)], axis=0)
    white, parts = pl.pallas_call(
        functools.partial(partial_kernel, bins),
        out_shape=[
            jax.ShapeDtypeStruct((rows, length), bf16),
            jax.ShapeDtypeStruct((bins, length, width), f32),
        ],
        compiler_params=params,
        name="partials",
    )(templates, code, gains, sketch)
    product = lax.psum_scatter(parts, "bin", scatter_dimension=0, tiled=True)[0]
    product = lax.psum(product, "grp")
    n = LANES
    halo = lax.ppermute(
        strain[:, -lead * n :], "grp", [(i, i + 1) for i in range(group_size - 1)]
    )
    xe = jnp.concatenate([halo, strain], axis=1).reshape(-1, n)
    basis, spectrum = pl.pallas_call(
        functools.partial(basis_kernel, scale),
        out_shape=[
            jax.ShapeDtypeStruct((length, width), bf16),
            jax.ShapeDtypeStruct((1, width), f32),
        ],
        scratch_shapes=[pltpu.VMEM((width, width), f32)] * 2,
        compiler_params=params,
        name="basis",
    )(product)
    bases = lax.all_gather(basis, "bin", axis=0, tiled=False)
    filtered = filters(xe, basis, lead, levels)
    mixing = pl.pallas_call(
        functools.partial(mixing_kernel, bins),
        out_shape=jax.ShapeDtypeStruct((rows, width), bf16),
        compiler_params=params,
        name="mixing",
    )(white, code, bases)
    return (mixing, spectrum, *filtered)


def solution(mesh):
    return jax.shard_map(
        functools.partial(local, mesh.shape["bin"], mesh.shape["grp"]),
        mesh=mesh,
        in_specs=(
            P(("bin", "grp"), None),
            P(("bin", "grp"), None),
            P(("bin", "grp")),
            P(),
            P(),
            P(None, "grp"),
        ),
        out_specs=(P(("bin", "grp"), None), P("bin", None)) + (P("bin", None, "grp", None),) * 5,
        check_vma=False,
    )
```

time: 496 us -> 226 us (0.46)
  matrix products: 179 us -> 0 us
  other arithmetic: 76.5 us -> 1.34 us
  local copies, waits for them, and re-layouts: 75.7 us -> 2.03 us
  Pallas kernels: 0 us -> 61.7 us
  waiting for transfers between devices: 105 us -> 141 us
  starting transfers between devices: 35.6 us -> 3.32 us
    conv_general_dilated x5 -> x0, matrix products: 166 us -> none  [filter_level(): lax.conv_general_dilated(joined[:, :, None], tap_rows[::-1][:, None, :],...]
    pallas_call x0 -> x4, Pallas kernels: none -> 61.7 us  [the longest x1 38.3 us: filters(): pl.pallas_call(functools.partial(filter_kernel, lead), out_shape=[jax.Sha...]
    another operation x12 -> x0, other arithmetic: 54.3 us -> none  [the longest x6 34.3 us: basis_from(): lower_factor = jnp.linalg.cholesky(inner_gram)]
    reduce_scatter x0 -> x1, waiting for transfers between devices: none -> 33.1 us  [local(): product = lax.psum_scatter(parts, 'bin', scatter_dimension=0, tiled=True)[0]]
    all_to_all x2 -> x0, starting transfers between devices: 20.4 us -> none  [the longest x1 12 us: local(): lax.all_to_all(outgoing, ('bin', 'grp'), split_axis=0, concat_axis=0, til...]
    broadcast_in_dim x15 -> x0, local copies, waits for them, and re-layouts: 16.2 us -> none  [the longest x5 15.2 us: local(): filtered.append(result_level.astype(jnp.bfloat16)[None])]
    convert_element_type x6 -> x0, local copies, waits for them, and re-layouts: 15.2 us -> none  [local(): filtered.append(result_level.astype(jnp.bfloat16)[None])]
    slice x15 -> x1, local copies, waits for them, and re-layouts: 13.3 us -> 0.01 us  [local(): strain[:, -lead * n:]]
  transfers between devices with their start and end apart: 8 -> 4, of which waited for: 2 -> 3; matrix products, arithmetic and copies ran while one was open for 47% -> 0% of each run, Pallas kernels for 0% -> 17%
where the time goes in v1:
time: 226 us; the launch traced here: 223 us
  waiting for transfers between devices  141 us (62%)
  Pallas kernels  61.7 us (27%)
  between operations  13.8 us (6%)
  starting transfers between devices  3.32 us (1%)
    psum x1, waiting for transfers between devices, local(): product = lax.psum(product, 'grp')  107 us
    pallas_call x1, Pallas kernels, filters(): pl.pallas_call(functools.partial(filter_kernel, lead), out_shape=[jax.Sha...  38.3 us
    reduce_scatter x1, waiting for transfers between devices, local(): product = lax.psum_scatter(parts, 'bin', scatter_dimension=0, tiled=True)[0]  33.1 us
    pallas_call x1, Pallas kernels, local(): pl.pallas_call(functools.partial(basis_kernel, scale), out_shape=[jax.Sha...  13.8 us
    pallas_call x1, Pallas kernels, local(): pl.pallas_call(functools.partial(partial_kernel, bins), out_shape=[jax.Sh...  5.94 us
  transfers between devices with their start and end apart: 4, of which 3 were waited for; matrix products, arithmetic and copies ran while one was open for 0% of the time, Pallas kernels for 17%

profile of v1, /device:TPU:1, one launch (start us, length us, event | category | flops | bytes accessed | tf_op | source)
XLA Modules:
  0.0 222.7 jit_solution(16689971094504896245)
XLA Ops:
  7.2 0.0 copy-start
  7.2 0.0 reduce-scatter.2.cloned.1.call-start
  7.2 1.3 fusion.2
  8.5 1.3 concatenate.6.gains_ref
  9.9 5.9 %partials.1 = (bf16[1024,512]{1,0:T(8,128)(2,1)}, f32[4,512,256]{2,1,0:T(8,128)}) custom-call(bf16[1024,512]{1,0:T(8,128)(2,1)} %t_ref.1, s32[1,1024]{1,0:T(1,128)} %bitcast.6, f32[8,512]{1,0:T(8,128)} %concatenate.6.gains_ref, f32[512,256]{1,0:T(8,128)} %sketch_ref.1), custom_call_target="tpu_custom_call" | custom-call | tf_op jit(solution)/shard_map/partials/pallas_call | solution.py:249
  15.8 0.0 reduce-scatter.2.cloned.1.call-update
  15.8 0.0 all-reduce.3.cloned.1.call-start
  15.9 33.1 %reduce-scatter.2.cloned.1.call-done = f32[1,512,256]{2,1,0:T(8,128)} async-done(((f32[4,512,256]{2,1,0:T(8,128)}), f32[1,512,256]{2,1,0:T(8,128)}) %reduce-scatter.2.cloned.1.call-update) | async-done | bytes 524304 | tf_op jit(solution)/shard_map/reduce_scatter | solution.py:258
  48.9 0.0 all-reduce.3.cloned.1.call-update
  49.0 0.2 all-gather.3.cloned.1.call-start
  49.2 106.7 %all-reduce.3.cloned.1.call-done.p_ref = f32[512,256]{1,0:T(8,128)} async-done(((f32[512,256]{1,0:T(8,128)}), f32[512,256]{1,0:T(8,128)}) %all-reduce.3.cloned.1.call-update) | async-done | bytes 524304 | tf_op jit(solution)/shard_map/psum | solution.py:259
  155.9 13.8 %basis.1 = (bf16[512,256]{1,0:T(8,128)(2,1)}, f32[1,256]{1,0:T(1,128)}) custom-call(f32[512,256]{1,0:T(8,128)} %all-reduce.3.cloned.1.call-done.p_ref), custom_call_target="tpu_custom_call" | custom-call | tf_op jit(solution)/shard_map/basis/pallas_call | solution.py:265
  169.7 0.0 all-gather.3.cloned.1.call-update
  169.7 0.0 copy-done
  169.8 3.0 %collective-permute-start = (f32[2,2048]{1,0:T(2,128)S(1)}, f32[2,2048]{1,0:T(2,128)S(1)}, u32[]{:S(2)}, u32[]{:S(2)}) collective-permute-start(f32[2,2048]{1,0:T(2,128)S(1)} %slice.3), channel_id=1, source_target_pairs={{0,1},{1,2},{2,3},{3,4},{4,5},{5,6},{6,7},{7,8},{8,9},{9,10},{10,1... | collective-permute-start | bytes 49160 | tf_op jit(solution)/shard_map/ppermute | solution.py:261
  172.8 0.6 collective-permute-done
  173.5 0.7 reshape.17.xe_ref
  174.2 38.3 %filters.1 = (bf16[1,2,8192,256]{3,2,1,0:T(8,128)(2,1)}, bf16[1,2,4096,256]{3,2,1,0:T(8,128)(2,1)}, bf16[1,2,2048,256]{3,2,1,0:T(8,128)(2,1)}, bf16[1,2,1024,256]{3,2,1,0:T(8,128)(2,1)}, bf16[1,2,512,256]{3,2,1,0:T(8,128)(2,1)}) custom-call(f32[160,128]{1,0:T(8,128)} %reshape.17.xe_ref, bf16[512,256]{1,0:T(8,128)(2,1)} %get-tuple-element.18.basis_ref), custom_call_target="tpu_custom_call" | custom-call | tf_op jit(solution)/shard_map/filters/pallas_call | solution.py:213
  212.5 0.0 all-gather.3.cloned.1.call-done
  212.5 3.7 %mixing.1 = bf16[1024,256]{1,0:T(8,128)(2,1)} custom-call(bf16[1024,512]{1,0:T(8,128)(2,1)} %get-tuple-element.16.white_ref, s32[1,1024]{1,0:T(1,128)} %bitcast.7, bf16[4,512,256]{2,1,0:T(8,128)(2,1)} %bitcast.4), custom_call_target="tpu_custom_call" | custom-call | tf_op jit(solution)/shard_map/mixing/pallas_call | solution.py:277
  (2 shorter events, 0.0 us)
Async XLA Ops:
  7.2 162.6 %copy-start = (f32[2,8192]{1,0:T(2,128)S(1)}, f32[2,8192]{1,0:T(2,128)}, u32[]{:S(2)}) copy-start(f32[2,8192]{1,0:T(2,128)} %param.11) | copy-start | bytes 196612
  7.2 41.8 %reduce-scatter.2.cloned.1.call-start = ((), (), s32[]{:S(2)}) async-start(), calls=%async_computation.1 | async-start | bytes 2621440 | tf_op jit(solution)/shard_map/reduce_scatter | solution.py:258
  15.8 140.1 %all-reduce.3.cloned.1.call-start = ((), (), s32[]{:S(2)}) async-start(), calls=%async_computation.2 | async-start | bytes 1048576 | tf_op jit(solution)/shard_map/psum | solution.py:259
  49.0 163.6 %all-gather.3.cloned.1.call-start = ((), (), s32[]{:S(2)}) async-start(), calls=%async_computation.3 | async-start | bytes 1310720 | tf_op jit(solution)/shard_map/all_gather | solution.py:275
  169.8 3.7 %collective-permute-start = (f32[2,2048]{1,0:T(2,128)S(1)}, f32[2,2048]{1,0:T(2,128)S(1)}, u32[]{:S(2)}, u32[]{:S(2)}) collective-permute-start(f32[2,2048]{1,0:T(2,128)S(1)} %slice.3), channel_id=1, source_target_pairs={{0,1},{1,2},{2,3},{3,4},{4,5},{5,6},{6,7},{7,8},{8,9},{9,10},{10,1... | collective-permute-start | bytes 49160 | tf_op jit(solution)/shard_map/ppermute | solution.py:261
Sparse Core Ops, SparseCore 0:
  15.9 32.9 reduce-scatter.1
  52.5 103.4 all-reduce.2
  169.9 22.7 all-gather.2

commit v2 on v1

--- a/solution.py
+++ b/solution.py
@@ -30,30 +30,192 @@
     return out
 
 
-def partial_kernel(bins, t_ref, code_ref, gains_ref, sketch_ref, white_ref, part_ref):
+def product_kernel(
+    bins, group_size, planes, lead,
+    t_ref, code_ref, gains_ref, sketch_ref, x_ref,
+    white_ref, product_ref, xe_ref,
+    halves, send1, recv1, send2, recv2, total, send3, recv3, full, edge, sems,
+):
     rows, length = t_ref.shape
-    width = sketch_ref.shape[1]
+    half = length // 2
+    piece = half // planes
+    bin_at, at = lax.axis_index("bin"), lax.axis_index("grp")
+    core, place = at % 2, at // 2
+    mesh_id = pl.DeviceIdType.MESH
+    sibling = (bin_at, place * 2 + 1 - core)
+    following = (bin_at, (at + 1) % group_size)
+    leading = (bin_at, (at + group_size - 1) % group_size)
+
+    barrier = pltpu.get_barrier_semaphore()
+
+    def greet(device):
+        pl.semaphore_signal(barrier, inc=1, device_id=device, device_id_type=mesh_id)
+
+    greet(sibling)
+    greet(following)
+    greet(leading)
+    for k in range(1, bins):
+        greet(((bin_at + k) % bins, at))
+
+    @pl.loop(1, planes)
+    def _(k):
+        greet((bin_at, (place + k) % planes * 2 + core))
+
+    def remote(src, dst, group, index, device):
+        return pltpu.make_async_remote_copy(
+            src_ref=src, dst_ref=dst, send_sem=sems.at[group, 0, index],
+            recv_sem=sems.at[group, 1, index], device_id=device, device_id_type=mesh_id,
+        )
+
     code = code_ref[...]
     rate = jnp.broadcast_to(code % 8, (24, rows))
     which = lax.broadcasted_iota(jnp.int32, (24, rows), 0) % 8
     onehot = jnp.where(rate == which, 1.0, 0.0).astype(bf16)
-    gains = gains_ref[...]
-    gains = jnp.concatenate(split(gains, 3), axis=0)
+    gains = jnp.concatenate(split(gains_ref[...], 3), axis=0)
     factor = dot(onehot, gains, 0, 0)
     white = (t_ref[...].astype(f32) * factor).astype(bf16)
     white_ref[...] = white
     sk = split(sketch_ref[...], 2)
     y = dot(white, sk[0], 1, 0) + dot(white, sk[1], 1, 0)
+    width = y.shape[1]
     bin_col = jnp.transpose(jnp.broadcast_to(code // 8, (8, rows)).astype(f32))[:, 0:1]
     yh, yl = split(y, 2)
     yh, yl = yh.astype(f32), yl.astype(f32)
-    for b in range(bins):
-        m = bin_col == float(b)
+
+    pl.semaphore_wait(barrier, planes + bins + 1)
+    xrows = x_ref.shape[0] // 2
+    edges = [
+        remote(x_ref.at[pl.ds(d * xrows + xrows - lead, lead), :], edge.at[d], 4, d, following)
+        for d in range(2)
+    ]
+    for e in edges:
+        e.start()
+
+    first = [remote(send1.at[k], recv1.at[k], 0, k, sibling) for k in range(bins)]
+    second = [
+        k and remote(send2.at[k], recv2.at[k], 1, k, ((bin_at + k) % bins, at))
+        for k in range(bins)
+    ]
+
+    def form(k):
+        m = bin_col == ((bin_at + k) % bins).astype(f32)
         yb = jnp.concatenate(
             [jnp.where(m, yh, 0.0).astype(bf16), jnp.where(m, yl, 0.0).astype(bf16)], axis=1
         )
         pb = dot(white, yb, 0, 0)
-        part_ref[b] = pb[:, :width] + pb[:, width:]
+        pb = pb[:, :width] + pb[:, width:]
+        halves[k, 0] = pb[:half]
+        halves[k, 1] = pb[half:]
+        send1[k] = halves[k, 1 - core].astype(bf16)
+        first[k].start()
+
+    def join(k):
+        first[k].wait_recv()
+        both = halves[k, core] + recv1[k].astype(f32)
+        if k:
+            send2[k] = both.astype(bf16)
+            second[k].start()
+        return both
+
+    form(1)
+    form(2)
+    join(1)
+    form(3)
+    join(2)
+    form(0)
+    join(3)
+    mine = join(0)
+    for k in range(1, bins):
+        second[k].wait_recv()
+        mine = mine + recv2[k].astype(f32)
+    total[...] = mine.reshape(planes, piece, width)
+    send3[...] = total[...].astype(bf16)
+
+    def third(k):
+        target = (place + k) % planes
+        return remote(send3.at[target], recv3.at[k], 2, k, (bin_at, target * 2 + core))
+
+    @pl.loop(1, planes)
+    def _(k):
+        third(k).start()
+
+    @pl.loop(1, planes)
+    def _(k):
+        third(k).wait_recv()
+
+    acc = total[place]
+    for k in range(1, planes):
+        acc = acc + recv3[k].astype(f32)
+    full[core, place] = acc
+
+    def fourth(k):
+        target = (place + k) % planes
+        return remote(
+            full.at[core, place], full.at[core, place], 3, k, (bin_at, target * 2 + core)
+        )
+
+    @pl.loop(1, planes)
+    def _(k):
+        fourth(k).start()
+
+    @pl.loop(1, planes)
+    def _(k):
+        fourth(k).wait_recv()
+
+    last = remote(full.at[core], full.at[core], 4, 2, sibling)
+    last.start()
+    for d in range(2):
+        edges[d].wait_recv()
+        xe_ref[pl.ds(d * (xrows + lead), lead), :] = jnp.where(at > 0, edge[d], 0.0)
+        xe_ref[pl.ds(d * (xrows + lead) + lead, xrows), :] = x_ref[pl.ds(d * xrows, xrows), :]
+        edges[d].wait_send()
+    for k in range(bins):
+        first[k].wait_send()
+    for k in range(1, bins):
+        second[k].wait_send()
+
+    @pl.loop(1, planes)
+    def _(k):
+        third(k).wait_send()
+        fourth(k).wait_send()
+
+    last.wait()
+    product_ref[...] = full[...].reshape(length, width)
+
+
+def products(bins, group_size, lead, templates, code, gains, sketch, x):
+    rows, length = templates.shape
+    width = sketch.shape[1]
+    planes = group_size // 2
+    half, piece = length // 2, length // group_size
+    vm = lambda: pl.BlockSpec(memory_space=pltpu.VMEM)
+    return pl.pallas_call(
+        functools.partial(product_kernel, bins, group_size, planes, lead),
+        out_shape=[
+            jax.ShapeDtypeStruct((rows, length), bf16),
+            jax.ShapeDtypeStruct((length, width), f32),
+            jax.ShapeDtypeStruct((x.shape[0] + 2 * lead, LANES), f32),
+        ],
+        in_specs=[vm() for _ in range(5)],
+        out_specs=[vm() for _ in range(3)],
+        scratch_shapes=[
+            pltpu.VMEM((bins, 2, half, width), f32),
+            pltpu.VMEM((bins, half, width), bf16),
+            pltpu.VMEM((bins, half, width), bf16),
+            pltpu.VMEM((bins, half, width), bf16),
+            pltpu.VMEM((bins, half, width), bf16),
+            pltpu.VMEM((planes, piece, width), f32),
+            pltpu.VMEM((planes, piece, width), bf16),
+            pltpu.VMEM((planes, piece, width), bf16),
+            pltpu.VMEM((2, planes, piece, width), f32),
+            pltpu.VMEM((2, lead, LANES), f32),
+            pltpu.SemaphoreType.DMA((5, 2, planes)),
+        ],
+        compiler_params=pltpu.CompilerParams(
+            vmem_limit_bytes=VMEM_LIMIT, collective_id=0, has_side_effects=True
+        ),
+        name="products",
+    )(templates, code, gains, sketch, x)
 
 
 def eliminate(D, nb, w=8):
@@ -246,22 +408,8 @@
     params = pltpu.CompilerParams(vmem_limit_bytes=VMEM_LIMIT)
     code = (owner_device[:, 0] // group_size * 8 + rate_code)[None, :]
     gains = jnp.concatenate([rate_gains, jnp.zeros((8 - levels, length), f32)], axis=0)
-    white, parts = pl.pallas_call(
-        functools.partial(partial_kernel, bins),
-        out_shape=[
-            jax.ShapeDtypeStruct((rows, length), bf16),
-            jax.ShapeDtypeStruct((bins, length, width), f32),
-        ],
-        compiler_params=params,
-        name="partials",
-    )(templates, code, gains, sketch)
-    product = lax.psum_scatter(parts, "bin", scatter_dimension=0, tiled=True)[0]
-    product = lax.psum(product, "grp")
-    n = LANES
-    halo = lax.ppermute(
-        strain[:, -lead * n :], "grp", [(i, i + 1) for i in range(group_size - 1)]
-    )
-    xe = jnp.concatenate([halo, strain], axis=1).reshape(-1, n)
+    x = strain.reshape(-1, LANES)
+    white, product, xe = products(bins, group_size, lead, templates, code, gains, sketch, x)
     basis, spectrum = pl.pallas_call(
         functools.partial(basis_kernel, scale),
         out_shape=[

time: 226 us -> 112 us (0.50); the launches traced: 223 us -> 111 us
  waiting for transfers between devices: 141 us -> 0.04 us
  Pallas kernels: 61.7 us -> 93.1 us
  starting transfers between devices: 3.32 us -> 0.04 us
    psum x1 -> x0, waiting for transfers between devices: 107 us -> none  [local(): product = lax.psum(product, 'grp')]
    reduce_scatter x1 -> x0, waiting for transfers between devices: 33.1 us -> none  [local(): product = lax.psum_scatter(parts, 'bin', scatter_dimension=0, tiled=True)[0]]
    pallas_call x1, Pallas kernels: 5.94 us -> 37.1 us  [products(): pl.pallas_call(functools.partial(product_kernel, bins, group_size, planes...]
    ppermute x1 -> x0, starting transfers between devices: 3.03 us -> none  [local(): lax.ppermute(strain[:, -lead * n:], 'grp', [(i, i + 1) for i in range(gro...]
  transfers between devices with their start and end apart: 4 -> 1, of which waited for: 3 -> 0; matrix products, arithmetic and copies ran while one was open for 0% -> 0% of each run, Pallas kernels for 17% -> 35%
where the time goes in v2:
time: 112 us; the launch traced here: 111 us
  Pallas kernels  93.1 us (83%)
  between operations  14.1 us (13%)
  local copies, waits for them, and re-layouts  2.85 us (3%)
  other arithmetic  1.3 us (1%)
    pallas_call x1, Pallas kernels, filters(): pl.pallas_call(functools.partial(filter_kernel, lead), out_shape=[jax.Sha...  38.6 us
    pallas_call x1, Pallas kernels, products(): pl.pallas_call(functools.partial(product_kernel, bins, group_size, planes...  37.1 us
    pallas_call x1, Pallas kernels, local(): pl.pallas_call(functools.partial(basis_kernel, scale), out_shape=[jax.Sha...  13.8 us
    pallas_call x1, Pallas kernels, local(): pl.pallas_call(functools.partial(mixing_kernel, bins), out_shape=jax.Shap...  3.65 us
  transfers between devices with their start and end apart: 1, of which 0 were waited for; matrix products, arithmetic and copies ran while one was open for 0% of the time, Pallas kernels for 35%

profile of v2, /device:TPU:1, one launch (start us, length us, event | category | flops | bytes accessed | tf_op | source)
XLA Modules:
  0.0 111.4 jit_solution(6035938157239955601)
XLA Ops:
  7.2 0.0 all-gather.3.cloned.1.call-start
  7.2 1.5 %reshape.17.x_ref = f32[128,128]{1,0:T(8,128)} reshape(f32[2,8192]{1,0:T(2,128)} %param.11) | data formatting | bytes 131072 | tf_op jit(solution)/shard_map/reshape | solution.py:411
  8.7 1.3 %fusion.2 = s32[1024]{0:T(1024)} fusion(s32[1024]{0:T(1024)} %param.8, s32[1024]{0:T(1024)} %bitcast.6), kind=kLoop, calls=%fused_computation.6 | loop fusion | flops 17408 | bytes 12288 | tf_op jit(solution)/shard_map/add | solution.py:409
  10.0 1.3 %concatenate.3.gains_ref = f32[8,512]{1,0:T(8,128)} pad(f32[5,512]{1,0:T(8,128)} %param.9, f32[]{:T(128)} %constant.19.clone.1), padding=0_3x0_0 | pad | bytes 26628 | tf_op jit(solution)/shard_map/concatenate | solution.py:410
  11.4 37.1 %products.1 = (bf16[1024,512]{1,0:T(8,128)(2,1)}, f32[512,256]{1,0:T(8,128)}, f32[160,128]{1,0:T(8,128)}) custom-call(bf16[1024,512]{1,0:T(8,128)(2,1)} %t_ref.1, s32[1,1024]{1,0:T(1,128)} %bitcast.4, f32[8,512]{1,0:T(8,128)} %concatenate.3.gains_ref, f32[512,256]{1,0:T(8,128)} %sketch_ref.1, f32[128,128]{1,0:T(8,128)} %reshape.17.x_ref), custom_call_target="tpu_custom_call" | custom-call | tf_op jit(solution)/shard_map/products/pallas_call | solution.py:192
  48.5 13.8 %basis.1 = (bf16[512,256]{1,0:T(8,128)(2,1)}, f32[1,256]{1,0:T(1,128)}) custom-call(f32[512,256]{1,0:T(8,128)} %get-tuple-element.18.p_ref), custom_call_target="tpu_custom_call" | custom-call | tf_op jit(solution)/shard_map/basis/pallas_call | solution.py:413
  62.3 0.0 all-gather.3.cloned.1.call-update
  62.3 38.6 %filters.1 = (bf16[1,2,8192,256]{3,2,1,0:T(8,128)(2,1)}, bf16[1,2,4096,256]{3,2,1,0:T(8,128)(2,1)}, bf16[1,2,2048,256]{3,2,1,0:T(8,128)(2,1)}, bf16[1,2,1024,256]{3,2,1,0:T(8,128)(2,1)}, bf16[1,2,512,256]{3,2,1,0:T(8,128)(2,1)}) custom-call(f32[160,128]{1,0:T(8,128)} %get-tuple-element.21.xe_ref, bf16[512,256]{1,0:T(8,128)(2,1)} %get-tuple-element.19.basis_ref), custom_call_target="tpu_custom_call" | custom-call | tf_op jit(solution)/shard_map/filters/pallas_call | solution.py:375
  100.8 0.0 all-gather.3.cloned.1.call-done
  100.9 3.7 %mixing.1 = bf16[1024,256]{1,0:T(8,128)(2,1)} custom-call(bf16[1024,512]{1,0:T(8,128)(2,1)} %get-tuple-element.17.white_ref, s32[1,1024]{1,0:T(1,128)} %bitcast.5, bf16[4,512,256]{2,1,0:T(8,128)(2,1)} %bitcast.3), custom_call_target="tpu_custom_call" | custom-call | tf_op jit(solution)/shard_map/mixing/pallas_call | solution.py:425
Async XLA Ops:
  7.2 93.7 %all-gather.3.cloned.1.call-start = ((), (), s32[]{:S(2)}) async-start(), calls=%async_computation | async-start | bytes 1310720 | tf_op jit(solution)/shard_map/all_gather | solution.py:423
Sparse Core Ops, SparseCore 0:
  62.4 20.9 all-gather.2

commit v3 on v2

--- a/solution.py
+++ b/solution.py
@@ -31,11 +31,12 @@
 
 
 def product_kernel(
-    bins, group_size, planes, lead,
+    bins, group_size, planes, lead, plan, levels,
     t_ref, code_ref, gains_ref, sketch_ref, x_ref,
-    white_ref, product_ref, xe_ref,
-    halves, send1, recv1, send2, recv2, total, send3, recv3, full, edge, sems,
+    white_ref, product_ref, strip_ref,
+    halves, send1, recv1, send2, recv2, total, send3, recv3, full, edge, xe, strip, *rest,
 ):
+    rvs, sems, strip_sem = rest[:levels], rest[levels], rest[levels + 1]
     rows, length = t_ref.shape
     half = length // 2
     piece = half // planes
@@ -71,7 +72,10 @@
     rate = jnp.broadcast_to(code % 8, (24, rows))
     which = lax.broadcasted_iota(jnp.int32, (24, rows), 0) % 8
     onehot = jnp.where(rate == which, 1.0, 0.0).astype(bf16)
-    gains = jnp.concatenate(split(gains_ref[...], 3), axis=0)
+    gains = jnp.concatenate(
+        [gains_ref[...], jnp.zeros((8 - levels, length), f32)], axis=0
+    )
+    gains = jnp.concatenate(split(gains, 3), axis=0)
     factor = dot(onehot, gains, 0, 0)
     white = (t_ref[...].astype(f32) * factor).astype(bf16)
     white_ref[...] = white
@@ -83,9 +87,16 @@
     yh, yl = yh.astype(f32), yl.astype(f32)
 
     pl.semaphore_wait(barrier, planes + bins + 1)
-    xrows = x_ref.shape[0] // 2
+    xrows = x_ref.shape[1] // LANES
+    for d in range(2):
+        for i in range(xrows):
+            xe[pl.ds(d * (xrows + lead) + lead + i, 1), :] = x_ref[
+                d : d + 1, i * LANES : (i + 1) * LANES
+            ]
     edges = [
-        remote(x_ref.at[pl.ds(d * xrows + xrows - lead, lead), :], edge.at[d], 4, d, following)
+        remote(
+            xe.at[pl.ds(d * (xrows + lead) + xrows, lead), :], edge.at[d], 4, d, following
+        )
         for d in range(2)
     ]
     for e in edges:
@@ -98,7 +109,7 @@
     ]
 
     def form(k):
-        m = bin_col == ((bin_at + k) % bins).astype(f32)
+        m = bin_col == float(k)
         yb = jnp.concatenate(
             [jnp.where(m, yh, 0.0).astype(bf16), jnp.where(m, yl, 0.0).astype(bf16)], axis=1
         )
@@ -125,6 +136,12 @@
     form(0)
     join(3)
     mine = join(0)
+    for d in range(2):
+        edges[d].wait_recv()
+        xe[pl.ds(d * (xrows + lead), lead), :] = jnp.where(at > 0, edge[d], 0.0)
+    decimate(rvs, xe[...])
+    for entry in plan[:2]:
+        build_strip(entry, rvs[entry[0]], strip)
     for k in range(1, bins):
         second[k].wait_recv()
         mine = mine + recv2[k].astype(f32)
@@ -139,6 +156,11 @@
     def _(k):
         third(k).start()
 
+    for entry in plan[2:]:
+        build_strip(entry, rvs[entry[0]], strip)
+    store = pltpu.make_async_copy(strip, strip_ref, strip_sem)
+    store.start()
+
     @pl.loop(1, planes)
     def _(k):
         third(k).wait_recv()
@@ -165,9 +187,6 @@
     last = remote(full.at[core], full.at[core], 4, 2, sibling)
     last.start()
     for d in range(2):
-        edges[d].wait_recv()
-        xe_ref[pl.ds(d * (xrows + lead), lead), :] = jnp.where(at > 0, edge[d], 0.0)
-        xe_ref[pl.ds(d * (xrows + lead) + lead, xrows), :] = x_ref[pl.ds(d * xrows, xrows), :]
         edges[d].wait_send()
     for k in range(bins):
         first[k].wait_send()
@@ -180,24 +199,27 @@
         fourth(k).wait_send()
 
     last.wait()
+    store.wait()
     product_ref[...] = full[...].reshape(length, width)
 
 
-def products(bins, group_size, lead, templates, code, gains, sketch, x):
+def products(bins, group_size, lead, plan, held, templates, code, gains, sketch, strain):
     rows, length = templates.shape
     width = sketch.shape[1]
+    levels = gains.shape[0]
     planes = group_size // 2
     half, piece = length // 2, length // group_size
+    xrows = strain.shape[1] // LANES + lead
     vm = lambda: pl.BlockSpec(memory_space=pltpu.VMEM)
     return pl.pallas_call(
-        functools.partial(product_kernel, bins, group_size, planes, lead),
+        functools.partial(product_kernel, bins, group_size, planes, lead, plan, levels),
         out_shape=[
             jax.ShapeDtypeStruct((rows, length), bf16),
             jax.ShapeDtypeStruct((length, width), f32),
-            jax.ShapeDtypeStruct((x.shape[0] + 2 * lead, LANES), f32),
+            jax.ShapeDtypeStruct((LANES, held * LANES), bf16),
         ],
         in_specs=[vm() for _ in range(5)],
-        out_specs=[vm() for _ in range(3)],
+        out_specs=[vm(), vm(), pl.BlockSpec(memory_space=pl.ANY)],
         scratch_shapes=[
             pltpu.VMEM((bins, 2, half, width), f32),
             pltpu.VMEM((bins, half, width), bf16),
@@ -209,13 +231,16 @@
             pltpu.VMEM((planes, piece, width), bf16),
             pltpu.VMEM((2, planes, piece, width), f32),
             pltpu.VMEM((2, lead, LANES), f32),
-            pltpu.SemaphoreType.DMA((5, 2, planes)),
-        ],
+            pltpu.VMEM((2 * xrows, LANES), f32),
+            pltpu.VMEM((LANES, held * LANES), bf16),
+        ]
+        + [pltpu.VMEM((2 * xrows >> r, LANES), f32) for r in range(levels)]
+        + [pltpu.SemaphoreType.DMA((5, 2, planes)), pltpu.SemaphoreType.DMA],
         compiler_params=pltpu.CompilerParams(
             vmem_limit_bytes=VMEM_LIMIT, collective_id=0, has_side_effects=True
         ),
         name="products",
-    )(templates, code, gains, sketch, x)
+    )(templates, code, gains, sketch, strain)
 
 
 def eliminate(D, nb, w=8):
@@ -280,26 +305,71 @@
     basis_ref[...] = basis_steps(p_ref[...], scale, A, X, spec_ref)
 
 
-def filter_kernel(lead, xe_ref, basis_ref, *rest):
-    outs, (rv0, rv1, rv2, rv3, rv4, bwide, strip), (o0, o1, o2, o3, o4), sems = (
-        rest[:5], rest[5:12], rest[12:17], rest[17]
-    )
-    rvs, obufs = (rv0, rv1, rv2, rv3, rv4), (o0, o1, o2, o3, o4)
-    levels = len(outs)
+def strip_plan(tiles, length, levels, lead):
+    plan, base = [], 0
+    for r in range(levels):
+        blocks = max(1, (length >> r) // LANES)
+        rows = (tiles + lead) >> r
+        held = (tiles >> r) + blocks - 1
+        chunk = next(m for m in (17, 16, 8, 4, 2, 1) if held % m == 0 or (m == 17 and held > 17 and held % 17 >= 15))
+        for d in range(2):
+            plan.append((r, d, tiles >> r, blocks, rows, chunk, -(-held // chunk), base))
+            base += -(-held // chunk) * chunk
+    return plan, base
+
+
+def decimate(rvs, x):
     n = LANES
     ri = lax.broadcasted_iota(jnp.int32, (n, n), 0)
     ci = lax.broadcasted_iota(jnp.int32, (n, n), 1)
     flip = jnp.where(ri + ci == n - 1, 1.0, 0.0).astype(f32)
     first = jnp.where(ri // 2 == ci, 1.0, 0.0).astype(f32)
     second = jnp.where(ri // 2 == ci - n // 2, 1.0, 0.0).astype(f32)
-    rv0[...] = dot(xe_ref[...], flip, 1, 0, highest)
-    for r in range(1, levels):
+    rvs[0][...] = dot(x, flip, 1, 0, highest)
+    for r in range(1, len(rvs)):
         count = rvs[r].shape[0]
         later = rvs[r - 1][pl.ds(1, count, stride=2), :]
         earlier = rvs[r - 1][pl.ds(0, count, stride=2), :]
         rvs[r][...] = (
             dot(later, first, 1, 0, highest) + dot(earlier, second, 1, 0, highest)
         ) * inv_root_two
+
+
+def build_strip(entry, rv, strip):
+    r, d, tiles, blocks, rows, chunk, count, base = entry
+    n = LANES
+    wide = chunk + 1
+    span = (wide + 1) * n
+
+    def step(i, carry):
+        q = d * rows + rows - 1 - i * chunk
+        z = jnp.concatenate(
+            [rv[pl.ds(jnp.maximum(q - j, 0), 1), :] for j in range(wide + 1)], axis=1
+        ).astype(bf16).astype(f32)
+        z = jnp.broadcast_to(z, (16, span))
+        z = pltpu.roll(z, span - 15, 1, stride=1, stride_axis=0)[:, : wide * n]
+        at = pl.ds(pl.multiple_of((base + i * chunk) * n, n), chunk * n)
+        for g in range(n // 16):
+            k = n - 16 - 16 * g
+            t = pltpu.roll(z, wide * n - k, 1) if k else z
+            strip[16 * g : 16 * g + 16, at] = t[:, : chunk * n].astype(bf16)
+        return carry
+
+    lax.fori_loop(0, count, step, 0)
+
+
+def filter_kernel(plan, levels, strip_ref, basis_ref, *rest):
+    outs, bwide, strip, obufs, in_sems, sems = (
+        rest[:levels], rest[levels], rest[levels + 1],
+        rest[levels + 2 : 2 * levels + 2], rest[-2], rest[-1],
+    )
+    n = LANES
+    length, width = basis_ref.shape
+    loads = []
+    for i, (r, d, tiles, blocks, rows, chunk, count, base) in enumerate(plan):
+        at = pl.ds(base * n, count * chunk * n)
+        loads.append(pltpu.make_async_copy(strip_ref.at[:, at], strip.at[:, at], in_sems.at[i]))
+        loads[-1].start()
     for h in range(bwide.shape[0]):
         bwide[h] = basis_ref[:, h * n : (h + 1) * n].astype(f32)
 
@@ -307,95 +377,70 @@
         halves = [bwide[h, pl.ds(0, taps, stride=step), :] for h in range(bwide.shape[0])]
         return jnp.concatenate(halves, axis=1)
 
-    length, width = basis_ref.shape
-    base = 0
-    copies = []
-    for r in range(levels):
+    for i, (r, d, tiles, blocks, rows, chunk, count, base) in enumerate(plan):
         taps = length >> r
-        blocks = max(1, taps // n)
-        rows = rvs[r].shape[0] // 2
-        head = lead >> r
-        tiles = rows - head
-        held = tiles + blocks - 1
-        if taps >= n:
-            weight = every(taps, 1 << r).astype(bf16) if r else basis_ref[...]
+        if r == 0:
+            weight = basis_ref[...]
+        elif taps >= n:
+            weight = every(taps, 1 << r).astype(bf16)
         else:
             weight = jnp.concatenate(
                 [every(taps, 1 << r), jnp.zeros((n - taps, width), f32)], axis=0
             ).astype(bf16)
-        bwide_r = weight
-        group = min(8, tiles)
-        for d in range(2):
-            first_col = base
-
-            def build(p, carry, r=r, d=d, rows=rows, first_col=first_col):
-                q = d * rows + rows - 1 - p
-                z = jnp.concatenate(
-                    [rvs[r][pl.ds(q, 1), :], rvs[r][pl.ds(q - 1, 1), :]], axis=1
-                ).astype(bf16).astype(f32)
-                z = jnp.broadcast_to(z, (n, 2 * n))
-                t = pltpu.roll(z, n + 1, 1, stride=1, stride_axis=0)[:, :n]
-                strip[:, pl.ds(pl.multiple_of((first_col + p) * n, n), n)] = t.astype(bf16)
-                return carry
-
-            lax.fori_loop(0, held, build, 0)
-
-            def tile(s, carry, r=r, d=d, rows=rows, first_col=first_col, group=group,
-                     blocks=blocks, weight=bwide_r, tiles=tiles):
-                parts = []
-                for i in range(group):
-                    p = first_col + tiles - 1 - (s * group + i)
-                    parts.append(strip[:, pl.ds(pl.multiple_of(p * n, n), blocks * n)])
-                lhs = jnp.concatenate(parts, axis=0)
-                span = group * n
-                obufs[r][d, pl.ds(pl.multiple_of(s * span, span), span), :] = dot(
-                    lhs, weight, 1, 0
-                ).astype(bf16)
-                pltpu.make_async_copy(
-                    obufs[r].at[d, pl.ds(pl.multiple_of(s * span, span), span), :],
-                    outs[r].at[0, d, pl.ds(pl.multiple_of(s * span, span), span), :],
-                    sems.at[r],
-                ).start()
-                return carry
-
-            lax.fori_loop(0, tiles // group, tile, 0)
-            base += held
+        group = min(32, tiles)
+        span = group * n
+        loads[i].wait()
+
+        def tile(s, carry, r=r, d=d, tiles=tiles, blocks=blocks, base=base, group=group, span=span,
+                 weight=weight):
+            parts = []
+            for t in range(group):
+                p = base + tiles - 1 - (s * group + t)
+                parts.append(strip[:, pl.ds(pl.multiple_of(p * n, n), blocks * n)])
+            at = pl.ds(pl.multiple_of(s * span, span), span)
+            obufs[r][d, at, :] = dot(jnp.concatenate(parts, axis=0), weight, 1, 0).astype(bf16)
+            pltpu.make_async_copy(
+                obufs[r].at[d, at, :], outs[r].at[0, d, at, :], sems.at[r]
+            ).start()
+            return carry
+
+        lax.fori_loop(0, tiles // group, tile, 0)
     for r in range(levels):
         pltpu.make_async_copy(obufs[r], outs[r].at[0], sems.at[r]).wait()
 
 
-def filters(xe, basis, lead, levels):
-    rows = xe.shape[0]
+def filters(plan, held, strip, basis, levels):
     length, width = basis.shape
-    samples = (rows // 2 - lead) * LANES
-    held = sum(
-        2 * ((samples >> r) // LANES + max(1, (length >> r) // LANES) - 1) for r in range(levels)
-    )
-    vm = lambda: pl.BlockSpec(memory_space=pltpu.VMEM)
+    samples = plan[0][2] * LANES
     return pl.pallas_call(
-        functools.partial(filter_kernel, lead),
+        functools.partial(filter_kernel, plan, levels),
         out_shape=[
             jax.ShapeDtypeStruct((1, 2, samples >> r, width), bf16) for r in range(levels)
         ],
-        in_specs=[vm(), vm()],
+        in_specs=[pl.BlockSpec(memory_space=pl.ANY), pl.BlockSpec(memory_space=pltpu.VMEM)],
         out_specs=[pl.BlockSpec(memory_space=pl.ANY)] * levels,
-        scratch_shapes=[pltpu.VMEM((rows >> r, LANES), f32) for r in range(levels)]
-        + [pltpu.VMEM((width // LANES, length, LANES), f32), pltpu.VMEM((LANES, held * LANES), bf16)]
+        scratch_shapes=[
+            pltpu.VMEM((width // LANES, length, LANES), f32),
+            pltpu.VMEM((LANES, held * LANES), bf16),
+        ]
         + [pltpu.VMEM((2, samples >> r, width), bf16) for r in range(levels)]
-        + [pltpu.SemaphoreType.DMA((levels,))],
+        + [pltpu.SemaphoreType.DMA((len(plan),)), pltpu.SemaphoreType.DMA((levels,))],
         compiler_params=pltpu.CompilerParams(vmem_limit_bytes=VMEM_LIMIT),
+        cost_estimate=pl.CostEstimate(
+            flops=2 * 2 * samples * length * width, bytes_accessed=26 << 20, transcendentals=0
+        ),
         name="filters",
-    )(xe, basis)
-
-
-def mixing_kernel(bins, white_ref, code_ref, bases_ref, out_ref):
+    )(strip, basis)
+
+
+def mixing_kernel(bins, white_ref, code_ref, *rest):
+    bases, out_ref = rest[:bins], rest[bins]
     rows = white_ref.shape[0]
     white = white_ref[...]
     bin_col = jnp.transpose(jnp.broadcast_to(code_ref[...] // 8, (8, rows)).astype(f32))[:, 0:1]
-    acc = None
-    for b in range(bins):
-        mixed = dot(white, bases_ref[b], 1, 0)
-        acc = mixed if acc is None else jnp.where(bin_col == float(b), mixed, acc)
+    acc = dot(white, bases[0][...], 1, 0)
+    for k in range(1, bins):
+        acc = jnp.where(bin_col == float(k), dot(white, bases[k][...], 1, 0), acc)
     out_ref[...] = acc.astype(bf16)
 
 
@@ -405,11 +450,13 @@
     levels = rate_gains.shape[0]
     lead = 16
     scale = 1.0 / (rows * group_size * math.sqrt(length))
-    params = pltpu.CompilerParams(vmem_limit_bytes=VMEM_LIMIT)
-    code = (owner_device[:, 0] // group_size * 8 + rate_code)[None, :]
-    gains = jnp.concatenate([rate_gains, jnp.zeros((8 - levels, length), f32)], axis=0)
-    x = strain.reshape(-1, LANES)
-    white, product, xe = products(bins, group_size, lead, templates, code, gains, sketch, x)
+    params = pltpu.CompilerParams(vmem_limit_bytes=24 << 20)
+    relative = (owner_device[:, 0] // group_size + bins - lax.axis_index("bin")) % bins
+    code = (relative * 8 + rate_code)[None, :]
+    plan, held = strip_plan(strain.shape[1] // LANES, length, levels, lead)
+    white, product, strip = products(
+        bins, group_size, lead, plan, held, templates, code, rate_gains, sketch, strain
+    )
     basis, spectrum = pl.pallas_call(
         functools.partial(basis_kernel, scale),
         out_shape=[
@@ -420,14 +467,17 @@
         compiler_params=params,
         name="basis",
     )(product)
-    bases = lax.all_gather(basis, "bin", axis=0, tiled=False)
-    filtered = filters(xe, basis, lead, levels)
+    others = [
+        lax.ppermute(basis, "bin", [(i, (i - k) % bins) for i in range(bins)])
+        for k in range(1, bins)
+    ]
+    filtered = filters(plan, held, strip, basis, levels)
     mixing = pl.pallas_call(
         functools.partial(mixing_kernel, bins),
         out_shape=jax.ShapeDtypeStruct((rows, width), bf16),
         compiler_params=params,
         name="mixing",
-    )(white, code, bases)
+    )(white, code, basis, *others)
     return (mixing, spectrum, *filtered)
 
 

time: 112 us -> 73.8 us (0.66)
  Pallas kernels: 93.1 us -> 65 us
  between operations: 14.1 us -> 0.72 us
  starting transfers between devices: 0.04 us -> 4.49 us
    pallas_call x1, Pallas kernels: 38.6 us -> 13.6 us  [filters(): pl.pallas_call(functools.partial(filter_kernel, plan, levels), out_shape=...]
    ppermute x0 -> x3, starting transfers between devices: none -> 4.49 us  [local(): lax.ppermute(basis, 'bin', [(i, (i - k) % bins) for i in range(bins)])]
    unnamed x0 -> x10, local copies, waits for them, and re-layouts: none -> 2.08 us
    pallas_call x1, Pallas kernels: 13.8 us -> 12.2 us  [local(): pl.pallas_call(functools.partial(basis_kernel, scale), out_shape=[jax.Sha...]
    pallas_call x1, Pallas kernels: 3.65 us -> 2.1 us  [local(): pl.pallas_call(functools.partial(mixing_kernel, bins), out_shape=jax.Shap...]
    reshape x1 -> x0, local copies, waits for them, and re-layouts: 1.53 us -> none  [local(): x = strain.reshape(-1, LANES)]
    concatenate x1 -> x0, local copies, waits for them, and re-layouts: 1.33 us -> none  [local(): jnp.concatenate([rate_gains, jnp.zeros((8 - levels, length), f32)], axis=0)]
  transfers between devices with their start and end apart: 1 -> 3, of which waited for: 0 -> 0; matrix products, arithmetic and copies ran while one was open for 0% -> 0% of each run, Pallas kernels for 35% -> 18%
where the time goes in v3:
time: 73.8 us; the launch traced here: 73.6 us
  Pallas kernels  65 us (88%)
  starting transfers between devices  4.49 us (6%)
  local copies, waits for them, and re-layouts  2.08 us (3%)
  other arithmetic  1.31 us (2%)
    pallas_call x1, Pallas kernels, products(): pl.pallas_call(functools.partial(product_kernel, bins, group_size, planes...  37.1 us
    pallas_call x1, Pallas kernels, filters(): pl.pallas_call(functools.partial(filter_kernel, plan, levels), out_shape=...  13.6 us
    pallas_call x1, Pallas kernels, local(): pl.pallas_call(functools.partial(basis_kernel, scale), out_shape=[jax.Sha...  12.2 us
    ppermute x3, starting transfers between devices, local(): lax.ppermute(basis, 'bin', [(i, (i - k) % bins) for i in range(bins)])  4.49 us
    pallas_call x1, Pallas kernels, local(): pl.pallas_call(functools.partial(mixing_kernel, bins), out_shape=jax.Shap...  2.1 us
    unnamed x10, local copies, waits for them, and re-layouts  2.08 us
  transfers between devices with their start and end apart: 3, of which 0 were waited for; matrix products, arithmetic and copies ran while one was open for 0% of the time, Pallas kernels for 18%

profile of v3, /device:TPU:1, one launch (start us, length us, event | category | flops | bytes accessed | tf_op | source)
XLA Modules:
  0.0 73.6 jit_solution(15457985869885505474)
XLA Ops:
  0.6 1.3 %fusion.5 = s32[1024]{0:T(1024)} fusion(s32[1024]{0:T(1024)} %param.8, s32[1024]{0:T(1024)} %bitcast.4, s32[]{:T(128)S(6)} %axis_index.15), kind=kLoop, calls=%fused_computation.12 | loop fusion | flops 30720 | bytes 12292 | tf_op jit(solution)/shard_map/add | solution.py:455
  1.9 37.1 %products.1 = (bf16[1024,512]{1,0:T(8,128)(2,1)}, f32[512,256]{1,0:T(8,128)}, bf16[128,33280]{1,0:T(8,128)(2,1)}) custom-call(bf16[1024,512]{1,0:T(8,128)(2,1)} %t_ref.1, s32[1,1024]{1,0:T(1,128)} %bitcast.2, f32[5,512]{1,0:T(8,128)} %gains_ref.1, f32[512,256]{1,0:T(8,128)} %sketch_ref.1, f32[2,8192]{1,0:T(2,128)} %x_ref.1), custom_call_target="tpu_custom_call" | custom-call | tf_op jit(solution)/shard_map/products/pallas_call | solution.py:214
  39.0 0.0 copy-start
  39.0 0.0 copy-start.1
  39.0 1.1 %copy-done.1 = f32[512,256]{1,0:T(8,128)S(1)} copy-done((f32[512,256]{1,0:T(8,128)S(1)}, f32[512,256]{1,0:T(8,128)}, u32[]{:S(2)}) %copy-start.1) | copy-done | bytes 524312
  40.2 0.0 copy-start.4
  40.2 12.2 %basis.1 = (bf16[512,256]{1,0:T(8,128)(2,1)S(1)}, f32[1,256]{1,0:T(1,128)}) custom-call(f32[512,256]{1,0:T(8,128)S(1)} %copy-done.1), custom_call_target="tpu_custom_call" | custom-call | tf_op jit(solution)/shard_map/basis/pallas_call | solution.py:460
  52.4 0.0 copy-start.2
  52.4 1.7 %collective-permute-start.2 = (bf16[512,256]{1,0:T(8,128)(2,1)S(1)}, bf16[512,256]{1,0:T(8,128)(2,1)S(1)}, u32[]{:S(2)}, u32[]{:S(2)}) collective-permute-start(bf16[512,256]{1,0:T(8,128)(2,1)S(1)} %get-tuple-element.19.rest_0_.basis_ref), channel_id=1, source_target_pairs={{0,32},{32,64},{64,96},{96,0},{1,33},{33,65},{65,97},{97,1},{2,34}... | collective-permute-start | bytes 786440 | tf_op jit(solution)/shard_map/ppermute | solution.py:471
  54.1 1.3 %collective-permute-start.1 = (bf16[512,256]{1,0:T(8,128)(2,1)S(1)}, bf16[512,256]{1,0:T(8,128)(2,1)S(1)}, u32[]{:S(2)}, u32[]{:S(2)}) collective-permute-start(bf16[512,256]{1,0:T(8,128)(2,1)S(1)} %get-tuple-element.19.rest_0_.basis_ref), channel_id=1, source_target_pairs={{0,64},{32,96},{64,0},{96,32},{1,65},{33,97},{65,1},{97,33},{2,66}... | collective-permute-start | bytes 786440 | tf_op jit(solution)/shard_map/ppermute | solution.py:471
  55.3 1.5 %collective-permute-start = (bf16[512,256]{1,0:T(8,128)(2,1)S(1)}, bf16[512,256]{1,0:T(8,128)(2,1)S(1)}, u32[]{:S(2)}, u32[]{:S(2)}) collective-permute-start(bf16[512,256]{1,0:T(8,128)(2,1)S(1)} %get-tuple-element.19.rest_0_.basis_ref), channel_id=1, source_target_pairs={{0,96},{32,0},{64,32},{96,64},{1,97},{33,1},{65,33},{97,65},{2,98}... | collective-permute-start | bytes 786440 | tf_op jit(solution)/shard_map/ppermute | solution.py:471
  56.9 0.0 copy-done.2
  56.9 13.6 %filters.1 = (bf16[1,2,8192,256]{3,2,1,0:T(8,128)(2,1)}, bf16[1,2,4096,256]{3,2,1,0:T(8,128)(2,1)}, bf16[1,2,2048,256]{3,2,1,0:T(8,128)(2,1)}, bf16[1,2,1024,256]{3,2,1,0:T(8,128)(2,1)}, bf16[1,2,512,256]{3,2,1,0:T(8,128)(2,1)}) custom-call(bf16[128,33280]{1,0:T(8,128)(2,1)} %get-tuple-element.21.strip_ref, bf16[512,256]{1,0:T(8,128)(2,1)} %copy-done.2), custom_call_target="tpu_custom_call" | custom-call | flops 4294967296 | bytes 27262976 | tf_op jit(solution)/shard_map/filters/pallas_call | solution.py:415
  70.5 0.0 collective-permute-done.2.rest_3_
  70.5 0.0 collective-permute-done.1.rest_2_
  70.5 0.0 collective-permute-done.rest_1_
  70.5 0.0 copy-done
  70.5 0.0 copy-done.4
  70.5 0.0 copy-start.3
  70.5 0.9 %copy-done.3 = bf16[512,256]{1,0:T(8,128)(2,1)S(1)} copy-done((bf16[512,256]{1,0:T(8,128)(2,1)S(1)}, bf16[512,256]{1,0:T(8,128)(2,1)}, u32[]{:S(2)}) %copy-start.3) | copy-done | bytes 262168
  71.5 2.1 %mixing.1 = bf16[1024,256]{1,0:T(8,128)(2,1)} custom-call(bf16[1024,512]{1,0:T(8,128)(2,1)S(1)} %copy-done, s32[1,1024]{1,0:T(1,128)S(1)} %bitcast.3, bf16[512,256]{1,0:T(8,128)(2,1)S(1)} %copy-done.3, bf16[512,256]{1,0:T(8,128)(2,1)S(1)} %collective-permute-done.rest_1_, bf16[512,256]{1,0:T(8,128)(2,1)S(1)} %collective-permute-done.1.rest_2_, ...), custom_call_target="tpu_custom_call" | custom-call | tf_op jit(solution)/shard_map/mixing/pallas_call | solution.py:475
Async XLA Ops:
  39.0 31.5 %copy-start = (bf16[1024,512]{1,0:T(8,128)(2,1)S(1)}, bf16[1024,512]{1,0:T(8,128)(2,1)}, u32[]{:S(2)}) copy-start(bf16[1024,512]{1,0:T(8,128)(2,1)} %get-tuple-element.17.white_ref) | copy-start | bytes 3145732
  39.0 1.1 %copy-start.1 = (f32[512,256]{1,0:T(8,128)S(1)}, f32[512,256]{1,0:T(8,128)}, u32[]{:S(2)}) copy-start(f32[512,256]{1,0:T(8,128)} %get-tuple-element.18.p_ref) | copy-start | bytes 1572868
  40.2 30.3 %copy-start.4 = (s32[1024]{0:T(1024)S(1)}, s32[1024]{0:T(1024)}, u32[]{:S(2)}) copy-start(s32[1024]{0:T(1024)} %fusion.5) | copy-start | bytes 12292
  52.4 4.5 %copy-start.2 = (bf16[512,256]{1,0:T(8,128)(2,1)}, bf16[512,256]{1,0:T(8,128)(2,1)S(1)}, u32[]{:S(2)}) copy-start(bf16[512,256]{1,0:T(8,128)(2,1)S(1)} %get-tuple-element.19.rest_0_.basis_ref) | copy-start | bytes 786436
  52.4 18.1 %collective-permute-start.2 = (bf16[512,256]{1,0:T(8,128)(2,1)S(1)}, bf16[512,256]{1,0:T(8,128)(2,1)S(1)}, u32[]{:S(2)}, u32[]{:S(2)}) collective-permute-start(bf16[512,256]{1,0:T(8,128)(2,1)S(1)} %get-tuple-element.19.rest_0_.basis_ref), channel_id=1, source_target_pairs={{0,32},{32,64},{64,96},{96,0},{1,33},{33,65},{65,97},{97,1},{2,34}... | collective-permute-start | bytes 786440 | tf_op jit(solution)/shard_map/ppermute | solution.py:471
  54.1 16.4 %collective-permute-start.1 = (bf16[512,256]{1,0:T(8,128)(2,1)S(1)}, bf16[512,256]{1,0:T(8,128)(2,1)S(1)}, u32[]{:S(2)}, u32[]{:S(2)}) collective-permute-start(bf16[512,256]{1,0:T(8,128)(2,1)S(1)} %get-tuple-element.19.rest_0_.basis_ref), channel_id=1, source_target_pairs={{0,64},{32,96},{64,0},{96,32},{1,65},{33,97},{65,1},{97,33},{2,66}... | collective-permute-start | bytes 786440 | tf_op jit(solution)/shard_map/ppermute | solution.py:471
  55.3 15.1 %collective-permute-start = (bf16[512,256]{1,0:T(8,128)(2,1)S(1)}, bf16[512,256]{1,0:T(8,128)(2,1)S(1)}, u32[]{:S(2)}, u32[]{:S(2)}) collective-permute-start(bf16[512,256]{1,0:T(8,128)(2,1)S(1)} %get-tuple-element.19.rest_0_.basis_ref), channel_id=1, source_target_pairs={{0,96},{32,0},{64,32},{96,64},{1,97},{33,1},{65,33},{97,65},{2,98}... | collective-permute-start | bytes 786440 | tf_op jit(solution)/shard_map/ppermute | solution.py:471
  70.5 1.0 %copy-start.3 = (bf16[512,256]{1,0:T(8,128)(2,1)S(1)}, bf16[512,256]{1,0:T(8,128)(2,1)}, u32[]{:S(2)}) copy-start(bf16[512,256]{1,0:T(8,128)(2,1)} %copy-done.2) | copy-start | bytes 786436

commit v4 on v3

--- a/solution.py
+++ b/solution.py
@@ -12,7 +12,6 @@
 highest = lax.Precision.HIGHEST
 inv_root_two = 0.7071067811865476
 LANES = 128
-VMEM_LIMIT = 56 << 20
 
 
 def dot(a, b, ca, cb, precision=None):
@@ -32,14 +31,16 @@
 
 def product_kernel(
     bins, group_size, planes, lead, plan, levels,
-    t_ref, code_ref, gains_ref, sketch_ref, x_ref,
-    white_ref, product_ref, strip_ref,
-    halves, send1, recv1, send2, recv2, total, send3, recv3, full, edge, xe, strip, *rest,
+    t_hbm, owner_hbm, rate_hbm, gains_hbm, sketch_hbm, x_hbm,
+    white_ref, product_ref, strip, bin_ref,
+    t_ref, owner_ref, rate_ref, gains_ref, sketch_ref, x_ref,
+    halves, send1, recv1, send2, recv2, sendv, recvv, total, send3, recv3, sendy, recvy,
+    full, edge, xe, *rest,
 ):
-    rvs, sems, strip_sem = rest[:levels], rest[levels], rest[levels + 1]
+    rvs, in_sems, sems = rest[:levels], rest[levels], rest[levels + 1]
     rows, length = t_ref.shape
     half = length // 2
-    piece = half // planes
+    part = half // planes // 2
     bin_at, at = lax.axis_index("bin"), lax.axis_index("grp")
     core, place = at % 2, at // 2
     mesh_id = pl.DeviceIdType.MESH
@@ -47,6 +48,17 @@
     following = (bin_at, (at + 1) % group_size)
     leading = (bin_at, (at + group_size - 1) % group_size)
 
+    loads = [
+        pltpu.make_async_copy(src, dst, in_sems.at[i])
+        for i, (src, dst) in enumerate(
+            [
+                (x_hbm, x_ref), (gains_hbm, gains_ref), (t_hbm, t_ref), (sketch_hbm, sketch_ref),
+                (owner_hbm, owner_ref), (rate_hbm, rate_ref),
+            ]
+        )
+    ]
+    for load in loads:
+        load.start()
     barrier = pltpu.get_barrier_semaphore()
 
     def greet(device):
@@ -68,34 +80,41 @@
             recv_sem=sems.at[group, 1, index], device_id=device, device_id_type=mesh_id,
         )
 
-    code = code_ref[...]
-    rate = jnp.broadcast_to(code % 8, (24, rows))
-    which = lax.broadcasted_iota(jnp.int32, (24, rows), 0) % 8
-    onehot = jnp.where(rate == which, 1.0, 0.0).astype(bf16)
-    gains = jnp.concatenate(
-        [gains_ref[...], jnp.zeros((8 - levels, length), f32)], axis=0
-    )
-    gains = jnp.concatenate(split(gains, 3), axis=0)
-    factor = dot(onehot, gains, 0, 0)
-    white = (t_ref[...].astype(f32) * factor).astype(bf16)
-    white_ref[...] = white
-    sk = split(sketch_ref[...], 2)
-    y = dot(white, sk[0], 1, 0) + dot(white, sk[1], 1, 0)
-    width = y.shape[1]
-    bin_col = jnp.transpose(jnp.broadcast_to(code // 8, (8, rows)).astype(f32))[:, 0:1]
-    yh, yl = split(y, 2)
-    yh, yl = yh.astype(f32), yl.astype(f32)
-
-    pl.semaphore_wait(barrier, planes + bins + 1)
+    loads[0].wait()
     xrows = x_ref.shape[1] // LANES
     for d in range(2):
         for i in range(xrows):
             xe[pl.ds(d * (xrows + lead) + lead + i, 1), :] = x_ref[
                 d : d + 1, i * LANES : (i + 1) * LANES
             ]
+    loads[1].wait()
+    gains = jnp.concatenate(
+        [gains_ref[...], jnp.zeros((8 - levels, length), f32)], axis=0
+    )
+    gains = jnp.concatenate(split(gains, 3), axis=0)
+    loads[4].wait()
+    loads[5].wait()
+    relative = (owner_ref[...] // group_size + bins - bin_at) % bins
+    bin_ref[...] = relative
+    bin_col = jnp.transpose(jnp.broadcast_to(relative, (8, rows)).astype(f32))[:, 0:1]
+    rate = jnp.broadcast_to(rate_ref[...], (24, rows))
+    which = lax.broadcasted_iota(jnp.int32, (24, rows), 0) % 8
+    onehot = jnp.where(rate == which, 1.0, 0.0).astype(bf16)
+    factor = dot(onehot, gains, 0, 0)
+    loads[2].wait()
+    white = (t_ref[...].astype(f32) * factor).astype(bf16)
+    white_ref[...] = white
+    loads[3].wait()
+    sk = split(sketch_ref[...], 2)
+    y = dot(white, sk[0], 1, 0) + dot(white, sk[1], 1, 0)
+    width = y.shape[1]
+    yh, yl = split(y, 2)
+    yh, yl = yh.astype(f32), yl.astype(f32)
+
+    pl.semaphore_wait(barrier, planes + bins + 1)
     edges = [
         remote(
-            xe.at[pl.ds(d * (xrows + lead) + xrows, lead), :], edge.at[d], 4, d, following
+            xe.at[pl.ds(d * (xrows + lead) + xrows, lead), :], edge.at[d], 4, bins + d, following
         )
         for d in range(2)
     ]
@@ -107,6 +126,27 @@
         k and remote(send2.at[k], recv2.at[k], 1, k, ((bin_at + k) % bins, at))
         for k in range(bins)
     ]
+    across = [
+        k and remote(sendy.at[k], recvy.at[k], 4, k, ((bin_at + k) % bins, at))
+        for k in range(bins)
+    ]
+
+    def spread(k):
+        target = (place + k) % planes
+        return remote(sendv.at[target], recvv.at[k], 2, k, (bin_at, target * 2 + core))
+
+    def third(k):
+        target = (place + k) % planes
+        return remote(send3.at[target], recv3.at[k], 3, k, (bin_at, target * 2 + core))
+
+    def fourth(k):
+        target = (place + k) % planes
+        mine = full.at[core, place]
+        return remote(mine, mine, 5, k, (bin_at, target * 2 + core))
+
+    def hand(k):
+        mine = full.at[core, (place + planes - k) % planes]
+        return remote(mine, mine, 6, k, sibling)
 
     def form(k):
         m = bin_col == float(k)
@@ -122,125 +162,154 @@
 
     def join(k):
         first[k].wait_recv()
-        both = halves[k, core] + recv1[k].astype(f32)
+        both = (halves[k, core] + recv1[k].astype(f32)).reshape(planes, 2, part, width)
         if k:
-            send2[k] = both.astype(bf16)
+            send2[k] = both[:, 0].astype(bf16)
             second[k].start()
-        return both
-
+        else:
+            total[...] = both[:, 0]
+        sendv[:, k] = both[:, 1].astype(bf16)
+
+    form(2)
     form(1)
-    form(2)
+    join(2)
+    form(3)
     join(1)
-    form(3)
-    join(2)
     form(0)
     join(3)
-    mine = join(0)
+    join(0)
+
+    @pl.loop(1, planes)
+    def _(k):
+        spread(k).start()
+
     for d in range(2):
         edges[d].wait_recv()
         xe[pl.ds(d * (xrows + lead), lead), :] = jnp.where(at > 0, edge[d], 0.0)
     decimate(rvs, xe[...])
-    for entry in plan[:2]:
+    for entry in plan[:1]:
         build_strip(entry, rvs[entry[0]], strip)
+
     for k in range(1, bins):
         second[k].wait_recv()
-        mine = mine + recv2[k].astype(f32)
-    total[...] = mine.reshape(planes, piece, width)
+        total[...] = total[...] + recv2[k].astype(f32)
     send3[...] = total[...].astype(bf16)
 
-    def third(k):
-        target = (place + k) % planes
-        return remote(send3.at[target], recv3.at[k], 2, k, (bin_at, target * 2 + core))
-
     @pl.loop(1, planes)
     def _(k):
         third(k).start()
+
+    @pl.loop(1, planes)
+    def _(k):
+        spread(k).wait_recv()
+
+    acc = sendv[place].astype(f32)
+    for k in range(1, planes):
+        acc = acc + recvv[k].astype(f32)
+    for k in range(1, bins):
+        sendy[k] = acc[k].astype(bf16)
+        across[k].start()
+
+    for entry in plan[1:2]:
+        build_strip(entry, rvs[entry[0]], strip)
+
+    @pl.loop(1, planes)
+    def _(k):
+        third(k).wait_recv()
+
+    one = total[place]
+    for k in range(1, planes):
+        one = one + recv3[k].astype(f32)
+    two = acc[0]
+    for k in range(1, bins):
+        across[k].wait_recv()
+        two = two + recvy[k].astype(f32)
+    full[core, place] = jnp.concatenate([one, two], axis=0)
+    hand(0).start()
+
+    @pl.loop(1, planes)
+    def _(k):
+        fourth(k).start()
 
     for entry in plan[2:]:
         build_strip(entry, rvs[entry[0]], strip)
-    store = pltpu.make_async_copy(strip, strip_ref, strip_sem)
-    store.start()
-
-    @pl.loop(1, planes)
-    def _(k):
-        third(k).wait_recv()
-
-    acc = total[place]
-    for k in range(1, planes):
-        acc = acc + recv3[k].astype(f32)
-    full[core, place] = acc
-
-    def fourth(k):
-        target = (place + k) % planes
-        return remote(
-            full.at[core, place], full.at[core, place], 3, k, (bin_at, target * 2 + core)
-        )
-
-    @pl.loop(1, planes)
-    def _(k):
-        fourth(k).start()
 
     @pl.loop(1, planes)
     def _(k):
         fourth(k).wait_recv()
-
-    last = remote(full.at[core], full.at[core], 4, 2, sibling)
-    last.start()
+        hand(k).start()
+
     for d in range(2):
         edges[d].wait_send()
     for k in range(bins):
         first[k].wait_send()
     for k in range(1, bins):
         second[k].wait_send()
-
-    @pl.loop(1, planes)
-    def _(k):
+        across[k].wait_send()
+
+    @pl.loop(1, planes)
+    def _(k):
+        spread(k).wait_send()
         third(k).wait_send()
         fourth(k).wait_send()
 
-    last.wait()
-    store.wait()
+    @pl.loop(0, planes)
+    def _(k):
+        hand(k).wait()
+
     product_ref[...] = full[...].reshape(length, width)
 
 
-def products(bins, group_size, lead, plan, held, templates, code, gains, sketch, strain):
+def products(bins, group_size, lead, plan, held, templates, owner, rate, gains, sketch, strain):
     rows, length = templates.shape
     width = sketch.shape[1]
     levels = gains.shape[0]
     planes = group_size // 2
-    half, piece = length // 2, length // group_size
+    half, part = length // 2, length // group_size // 2
+    hbm = lambda: pl.BlockSpec(memory_space=pltpu.HBM)
     xrows = strain.shape[1] // LANES + lead
     vm = lambda: pl.BlockSpec(memory_space=pltpu.VMEM)
+    far = lambda a: pltpu.with_memory_space_constraint(a, pltpu.HBM)
     return pl.pallas_call(
         functools.partial(product_kernel, bins, group_size, planes, lead, plan, levels),
         out_shape=[
             jax.ShapeDtypeStruct((rows, length), bf16),
             jax.ShapeDtypeStruct((length, width), f32),
             jax.ShapeDtypeStruct((LANES, held * LANES), bf16),
+            jax.ShapeDtypeStruct((1, rows), jnp.int32),
         ],
-        in_specs=[vm() for _ in range(5)],
-        out_specs=[vm(), vm(), pl.BlockSpec(memory_space=pl.ANY)],
+        in_specs=[hbm() for _ in range(6)],
+        out_specs=[vm() for _ in range(4)],
         scratch_shapes=[
+            pltpu.VMEM(templates.shape, bf16),
+            pltpu.VMEM(owner.shape, jnp.int32),
+            pltpu.VMEM(rate.shape, jnp.int32),
+            pltpu.VMEM(gains.shape, f32),
+            pltpu.VMEM(sketch.shape, f32),
+            pltpu.VMEM(strain.shape, f32),
             pltpu.VMEM((bins, 2, half, width), f32),
             pltpu.VMEM((bins, half, width), bf16),
             pltpu.VMEM((bins, half, width), bf16),
-            pltpu.VMEM((bins, half, width), bf16),
-            pltpu.VMEM((bins, half, width), bf16),
-            pltpu.VMEM((planes, piece, width), f32),
-            pltpu.VMEM((planes, piece, width), bf16),
-            pltpu.VMEM((planes, piece, width), bf16),
-            pltpu.VMEM((2, planes, piece, width), f32),
+            pltpu.VMEM((bins, planes, part, width), bf16),
+            pltpu.VMEM((bins, planes, part, width), bf16),
+            pltpu.VMEM((planes, bins, part, width), bf16),
+            pltpu.VMEM((planes, bins, part, width), bf16),
+            pltpu.VMEM((planes, part, width), f32),
+            pltpu.VMEM((planes, part, width), bf16),
+            pltpu.VMEM((planes, part, width), bf16),
+            pltpu.VMEM((bins, part, width), bf16),
+            pltpu.VMEM((bins, part, width), bf16),
+            pltpu.VMEM((2, planes, 2 * part, width), f32),
             pltpu.VMEM((2, lead, LANES), f32),
             pltpu.VMEM((2 * xrows, LANES), f32),
-            pltpu.VMEM((LANES, held * LANES), bf16),
         ]
         + [pltpu.VMEM((2 * xrows >> r, LANES), f32) for r in range(levels)]
-        + [pltpu.SemaphoreType.DMA((5, 2, planes)), pltpu.SemaphoreType.DMA],
+        + [pltpu.SemaphoreType.DMA((6,)), pltpu.SemaphoreType.DMA((7, 2, planes))],
         compiler_params=pltpu.CompilerParams(
-            vmem_limit_bytes=VMEM_LIMIT, collective_id=0, has_side_effects=True
+            vmem_limit_bytes=30 << 20, collective_id=0, has_side_effects=True
         ),
         name="products",
-    )(templates, code, gains, sketch, strain)
+    )(far(templates), far(owner), far(rate), far(gains), far(sketch), far(strain))
 
 
 def eliminate(D, nb, w=8):
@@ -358,18 +427,12 @@
     lax.fori_loop(0, count, step, 0)
 
 
-def filter_kernel(plan, levels, strip_ref, basis_ref, *rest):
-    outs, bwide, strip, obufs, in_sems, sems = (
-        rest[:levels], rest[levels], rest[levels + 1],
-        rest[levels + 2 : 2 * levels + 2], rest[-2], rest[-1],
+def filter_kernel(plan, levels, strip, basis_ref, *rest):
+    outs, bwide, obufs, sems = (
+        rest[:levels], rest[levels], rest[levels + 1 : 2 * levels + 1], rest[-1]
     )
     n = LANES
     length, width = basis_ref.shape
-    loads = []
-    for i, (r, d, tiles, blocks, rows, chunk, count, base) in enumerate(plan):
-        at = pl.ds(base * n, count * chunk * n)
-        loads.append(pltpu.make_async_copy(strip_ref.at[:, at], strip.at[:, at], in_sems.at[i]))
-        loads[-1].start()
     for h in range(bwide.shape[0]):
         bwide[h] = basis_ref[:, h * n : (h + 1) * n].astype(f32)
 
@@ -377,7 +440,7 @@
         halves = [bwide[h, pl.ds(0, taps, stride=step), :] for h in range(bwide.shape[0])]
         return jnp.concatenate(halves, axis=1)
 
-    for i, (r, d, tiles, blocks, rows, chunk, count, base) in enumerate(plan):
+    for r, d, tiles, blocks, rows, chunk, count, base in plan:
         taps = length >> r
         if r == 0:
             weight = basis_ref[...]
@@ -389,7 +452,6 @@
             ).astype(bf16)
         group = min(32, tiles)
         span = group * n
-        loads[i].wait()
 
         def tile(s, carry, r=r, d=d, tiles=tiles, blocks=blocks, base=base, group=group, span=span,
                  weight=weight):
@@ -417,15 +479,12 @@
         out_shape=[
             jax.ShapeDtypeStruct((1, 2, samples >> r, width), bf16) for r in range(levels)
         ],
-        in_specs=[pl.BlockSpec(memory_space=pl.ANY), pl.BlockSpec(memory_space=pltpu.VMEM)],
+        in_specs=[pl.BlockSpec(memory_space=pltpu.VMEM)] * 2,
         out_specs=[pl.BlockSpec(memory_space=pl.ANY)] * levels,
-        scratch_shapes=[
-            pltpu.VMEM((width // LANES, length, LANES), f32),
-            pltpu.VMEM((LANES, held * LANES), bf16),
-        ]
+        scratch_shapes=[pltpu.VMEM((width // LANES, length, LANES), f32)]
         + [pltpu.VMEM((2, samples >> r, width), bf16) for r in range(levels)]
-        + [pltpu.SemaphoreType.DMA((len(plan),)), pltpu.SemaphoreType.DMA((levels,))],
-        compiler_params=pltpu.CompilerParams(vmem_limit_bytes=VMEM_LIMIT),
+        + [pltpu.SemaphoreType.DMA((levels,))],
+        compiler_params=pltpu.CompilerParams(vmem_limit_bytes=40 << 20),
         cost_estimate=pl.CostEstimate(
             flops=2 * 2 * samples * length * width, bytes_accessed=26 << 20, transcendentals=0
         ),
@@ -433,11 +492,11 @@
     )(strip, basis)
 
 
-def mixing_kernel(bins, white_ref, code_ref, *rest):
+def mixing_kernel(bins, white_ref, bin_ref, *rest):
     bases, out_ref = rest[:bins], rest[bins]
     rows = white_ref.shape[0]
     white = white_ref[...]
-    bin_col = jnp.transpose(jnp.broadcast_to(code_ref[...] // 8, (8, rows)).astype(f32))[:, 0:1]
+    bin_col = jnp.transpose(jnp.broadcast_to(bin_ref[...], (8, rows)).astype(f32))[:, 0:1]
     acc = dot(white, bases[0][...], 1, 0)
     for k in range(1, bins):
         acc = jnp.where(bin_col == float(k), dot(white, bases[k][...], 1, 0), acc)
@@ -451,11 +510,10 @@
     lead = 16
     scale = 1.0 / (rows * group_size * math.sqrt(length))
     params = pltpu.CompilerParams(vmem_limit_bytes=24 << 20)
-    relative = (owner_device[:, 0] // group_size + bins - lax.axis_index("bin")) % bins
-    code = (relative * 8 + rate_code)[None, :]
     plan, held = strip_plan(strain.shape[1] // LANES, length, levels, lead)
-    white, product, strip = products(
-        bins, group_size, lead, plan, held, templates, code, rate_gains, sketch, strain
+    white, product, strip, relative = products(
+        bins, group_size, lead, plan, held, templates, owner_device.reshape(1, rows),
+        rate_code.reshape(1, rows), rate_gains, sketch, strain,
     )
     basis, spectrum = pl.pallas_call(
         functools.partial(basis_kernel, scale),
@@ -477,7 +535,7 @@
         out_shape=jax.ShapeDtypeStruct((rows, width), bf16),
         compiler_params=params,
         name="mixing",
-    )(white, code, basis, *others)
+    )(white, relative, basis, *others)
     return (mixing, spectrum, *filtered)
 
 

time: 73.8 us -> 64.3 us (0.87)
  Pallas kernels: 65 us -> 58.2 us
  waiting for transfers between devices: 0.01 us -> 2.23 us
  local copies, waits for them, and re-layouts: 2.08 us -> 0 us
  starting transfers between devices: 4.49 us -> 3.07 us
  other arithmetic: 1.31 us -> 0 us
    pallas_call x1, Pallas kernels: 13.6 us -> 9.58 us  [filters(): pl.pallas_call(functools.partial(filter_kernel, plan, levels), out_shape=...]
    pallas_call x1, Pallas kernels: 37.1 us -> 34.4 us  [products(): pl.pallas_call(functools.partial(product_kernel, bins, group_size, planes...]
    ppermute x3, waiting for transfers between devices: 0.01 us -> 2.23 us  [local(): lax.ppermute(basis, 'bin', [(i, (i - k) % bins) for i in range(bins)])]
    unnamed x10 -> x0, local copies, waits for them, and re-layouts: 2.08 us -> none
    ppermute x3, starting transfers between devices: 4.49 us -> 3.07 us  [local(): lax.ppermute(basis, 'bin', [(i, (i - k) % bins) for i in range(bins)])]
    add x1 -> x0, other arithmetic: 1.31 us -> none  [local(): code = (relative * 8 + rate_code)[None, :]]
  transfers between devices with their start and end apart: 3 -> 3, of which waited for: 0 -> 2; matrix products, arithmetic and copies ran while one was open for 0% -> 0% of each run, Pallas kernels for 18% -> 15%
where the time goes in v4:
time: 64.3 us; the launch traced here: 64.2 us
  Pallas kernels  58.2 us (91%)
  starting transfers between devices  3.07 us (5%)
  waiting for transfers between devices  2.23 us (3%)
  between operations  0.65 us (1%)
    pallas_call x1, Pallas kernels, products(): pl.pallas_call(functools.partial(product_kernel, bins, group_size, planes...  34.4 us
    pallas_call x1, Pallas kernels, local(): pl.pallas_call(functools.partial(basis_kernel, scale), out_shape=[jax.Sha...  12.2 us
    pallas_call x1, Pallas kernels, filters(): pl.pallas_call(functools.partial(filter_kernel, plan, levels), out_shape=...  9.58 us
    ppermute x3, starting transfers between devices, local(): lax.ppermute(basis, 'bin', [(i, (i - k) % bins) for i in range(bins)])  3.07 us
    ppermute x3, waiting for transfers between devices, local(): lax.ppermute(basis, 'bin', [(i, (i - k) % bins) for i in range(bins)])  2.23 us
    pallas_call x1, Pallas kernels, local(): pl.pallas_call(functools.partial(mixing_kernel, bins), out_shape=jax.Shap...  2.05 us
  transfers between devices with their start and end apart: 3, of which 2 were waited for; matrix products, arithmetic and copies ran while one was open for 0% of the time, Pallas kernels for 15%

profile of v4, /device:TPU:1, one launch (start us, length us, event | category | flops | bytes accessed | tf_op | source)
XLA Modules:
  0.0 64.2 jit_solution(14077355811663928518)
XLA Ops:
  0.6 34.4 %products.1 = (bf16[1024,512]{1,0:T(8,128)(2,1)S(1)}, f32[512,256]{1,0:T(8,128)S(1)}, bf16[128,33280]{1,0:T(8,128)(2,1)S(1)}, s32[1,1024]{1,0:T(1,128)S(1)}) custom-call(bf16[1024,512]{1,0:T(8,128)(2,1)} %t_hbm.1, s32[1,1024]{1,0:T(1,128)} %bitcast.2, s32[1,1024]{1,0:T(1,128)} %bitcast.3, f32[5,512]{1,0:T(8,128)} %gains_hbm.1, f32[512,256]{1,0:T(8,128)} %sketch_hbm.1, ...), custom_call_target="tpu_custom_call" | custom-call | tf_op jit(solution)/shard_map/products/pallas_call | solution.py:273
  35.1 12.2 %basis.1 = (bf16[512,256]{1,0:T(8,128)(2,1)S(1)}, f32[1,256]{1,0:T(1,128)}) custom-call(f32[512,256]{1,0:T(8,128)S(1)} %get-tuple-element.20.p_ref), custom_call_target="tpu_custom_call" | custom-call | tf_op jit(solution)/shard_map/basis/pallas_call | solution.py:518
  47.3 0.4 collective-permute-start.2
  47.6 1.4 %collective-permute-start.1 = (bf16[512,256]{1,0:T(8,128)(2,1)S(1)}, bf16[512,256]{1,0:T(8,128)(2,1)S(1)}, u32[]{:S(2)}, u32[]{:S(2)}) collective-permute-start(bf16[512,256]{1,0:T(8,128)(2,1)S(1)} %get-tuple-element.21.rest_0_.basis_ref), channel_id=1, source_target_pairs={{0,64},{32,96},{64,0},{96,32},{1,65},{33,97},{65,1},{97,33},{2,66}... | collective-permute-start | bytes 786440 | tf_op jit(solution)/shard_map/ppermute | solution.py:529
  49.0 1.3 %collective-permute-start = (bf16[512,256]{1,0:T(8,128)(2,1)S(1)}, bf16[512,256]{1,0:T(8,128)(2,1)S(1)}, u32[]{:S(2)}, u32[]{:S(2)}) collective-permute-start(bf16[512,256]{1,0:T(8,128)(2,1)S(1)} %get-tuple-element.21.rest_0_.basis_ref), channel_id=1, source_target_pairs={{0,96},{32,0},{64,32},{96,64},{1,97},{33,1},{65,33},{97,65},{2,98}... | collective-permute-start | bytes 786440 | tf_op jit(solution)/shard_map/ppermute | solution.py:529
  50.3 9.6 %filters.1 = (bf16[1,2,8192,256]{3,2,1,0:T(8,128)(2,1)}, bf16[1,2,4096,256]{3,2,1,0:T(8,128)(2,1)}, bf16[1,2,2048,256]{3,2,1,0:T(8,128)(2,1)}, bf16[1,2,1024,256]{3,2,1,0:T(8,128)(2,1)}, bf16[1,2,512,256]{3,2,1,0:T(8,128)(2,1)}) custom-call(bf16[128,33280]{1,0:T(8,128)(2,1)S(1)} %get-tuple-element.23.strip, ...), custom_call_target="tpu_custom_call" | custom-call | flops 4294967296 | bytes 27262976 | tf_op jit(solution)/shard_map/filters/pallas_call | solution.py:477
  59.9 1.9 %collective-permute-done.2.rest_3_ = bf16[512,256]{1,0:T(8,128)(2,1)S(1)} collective-permute-done((bf16[512,256]{1,0:T(8,128)(2,1)S(1)}, bf16[512,256]{1,0:T(8,128)(2,1)S(1)}, u32[]{:S(2)}, u32[]{:S(2)}) %collective-permute-start.2) | collective-permute-done | bytes 262176 | tf_op jit(solution)/shard_map/ppermute | solution.py:529
  61.8 0.0 collective-permute-done.1.rest_2_
  61.9 0.3 collective-permute-done.rest_1_
  62.2 2.0 %mixing.1 = bf16[1024,256]{1,0:T(8,128)(2,1)} custom-call(bf16[1024,512]{1,0:T(8,128)(2,1)S(1)} %get-tuple-element.18.white_ref, s32[1,1024]{1,0:T(1,128)S(1)} %get-tuple-element.19.bin_ref, bf16[512,256]{1,0:T(8,128)(2,1)S(1)} %get-tuple-element.21.rest_0_.basis_ref, bf16[512,256]{1,0:T(8,128)(2,1)S(1)} %collective-permute-done.rest_1_, ...), custom_call_target="tpu_custom_call" | custom-call | tf_op jit(solution)/shard_map/mixing/pallas_call | solution.py:533
Async XLA Ops:
  47.3 14.6 %collective-permute-start.2 = (bf16[512,256]{1,0:T(8,128)(2,1)S(1)}, bf16[512,256]{1,0:T(8,128)(2,1)S(1)}, u32[]{:S(2)}, u32[]{:S(2)}) collective-permute-start(bf16[512,256]{1,0:T(8,128)(2,1)S(1)} %get-tuple-element.21.rest_0_.basis_ref), channel_id=1, source_target_pairs={{0,32},{32,64},{64,96},{96,0},{1,33},{33,65},{65,97},{97,1},{2,34}... | collective-permute-start | bytes 786440 | tf_op jit(solution)/shard_map/ppermute | solution.py:529
  47.6 14.2 %collective-permute-start.1 = (bf16[512,256]{1,0:T(8,128)(2,1)S(1)}, bf16[512,256]{1,0:T(8,128)(2,1)S(1)}, u32[]{:S(2)}, u32[]{:S(2)}) collective-permute-start(bf16[512,256]{1,0:T(8,128)(2,1)S(1)} %get-tuple-element.21.rest_0_.basis_ref), channel_id=1, source_target_pairs={{0,64},{32,96},{64,0},{96,32},{1,65},{33,97},{65,1},{97,33},{2,66}... | collective-permute-start | bytes 786440 | tf_op jit(solution)/shard_map/ppermute | solution.py:529
  49.0 13.1 %collective-permute-start = (bf16[512,256]{1,0:T(8,128)(2,1)S(1)}, bf16[512,256]{1,0:T(8,128)(2,1)S(1)}, u32[]{:S(2)}, u32[]{:S(2)}) collective-permute-start(bf16[512,256]{1,0:T(8,128)(2,1)S(1)} %get-tuple-element.21.rest_0_.basis_ref), channel_id=1, source_target_pairs={{0,96},{32,0},{64,32},{96,64},{1,97},{33,1},{65,33},{97,65},{2,98}... | collective-permute-start | bytes 786440 | tf_op jit(solution)/shard_map/ppermute | solution.py:529

commit v5 on v4

v5 whole, which is shorter than its diff:
```python
import functools
import math

import jax
import jax.numpy as jnp
from jax import lax
from jax.experimental import pallas as pl
from jax.experimental.pallas import tpu as pltpu
from jax.sharding import PartitionSpec as P

f32, bf16 = jnp.float32, jnp.bfloat16
highest = lax.Precision.HIGHEST
inv_root_two = 0.7071067811865476
LANES = 128


def dot(a, b, ca, cb, precision=None):
    return lax.dot_general(
        a, b, (((ca,), (cb,)), ((), ())), precision=precision, preferred_element_type=f32
    )


def split(x, parts):
    out = []
    for _ in range(parts):
        piece = x.astype(bf16)
        out.append(piece)
        x = x - piece.astype(f32)
    return out


def product_kernel(
    bins, group_size, planes, lead, plan, levels,
    t_hbm, owner_hbm, rate_hbm, gains_hbm, sketch_hbm, x_hbm,
    white_ref, product_ref, strip, bin_ref,
    t_ref, owner_ref, rate_ref, gains_ref, sketch_ref, x_ref, turned,
    halves, send1, recv1, send2, recv2, sendv, recvv, total, send3, recv3, sendy, recvy,
    full, edge, xe, *rest,
):
    rvs, in_sems, sems = rest[:levels], rest[levels], rest[levels + 1]
    rows, length = t_ref.shape
    half = length // 2
    part = half // planes // 2
    bin_at, at = lax.axis_index("bin"), lax.axis_index("grp")
    core, place = at & 1, at >> 1
    mesh_id = pl.DeviceIdType.MESH
    sibling = (bin_at, place * 2 + 1 - core)
    following = (bin_at, (at + 1) & (group_size - 1))
    leading = (bin_at, (at - 1) & (group_size - 1))

    def fellow(k):
        return ((place + k) & (planes - 1)) * 2 + core

    def other(k):
        return ((bin_at + k) & (bins - 1), at)

    loads = [
        pltpu.make_async_copy(src, dst, in_sems.at[i])
        for i, (src, dst) in enumerate(
            [
                (x_hbm, x_ref), (gains_hbm, gains_ref), (t_hbm, t_ref), (sketch_hbm, sketch_ref),
                (owner_hbm, owner_ref), (rate_hbm, rate_ref),
            ]
        )
    ]
    for load in loads:
        load.start()
    barrier = pltpu.get_barrier_semaphore()

    def greet(device):
        pl.semaphore_signal(barrier, inc=1, device_id=device, device_id_type=mesh_id)

    greet(sibling)
    greet(following)
    greet(leading)
    for k in range(1, bins):
        greet(other(k))

    @pl.loop(1, planes, unroll=True)
    def _(k):
        greet((bin_at, fellow(k)))

    def remote(src, dst, group, index, device):
        return pltpu.make_async_remote_copy(
            src_ref=src, dst_ref=dst, send_sem=sems.at[group, 0, index],
            recv_sem=sems.at[group, 1, index], device_id=device, device_id_type=mesh_id,
        )

    loads[1].wait()
    gains = jnp.concatenate(
        [gains_ref[...], jnp.zeros((8 - levels, length), f32)], axis=0
    )
    gains = jnp.concatenate(split(gains, 3), axis=0)
    loads[4].wait()
    loads[5].wait()
    shift = group_size.bit_length() - 1
    relative = ((owner_ref[...] >> shift) - bin_at) & (bins - 1)
    bin_ref[...] = relative
    bin_col = jnp.transpose(jnp.broadcast_to(relative, (8, rows)).astype(f32))[:, 0:1]
    rate = jnp.broadcast_to(rate_ref[...], (24, rows))
    which = lax.broadcasted_iota(jnp.int32, (24, rows), 0) % 8
    onehot = jnp.where(rate == which, 1.0, 0.0).astype(bf16)
    factor = dot(onehot, gains, 0, 0)
    loads[2].wait()
    white = (t_ref[...].astype(f32) * factor).astype(bf16)
    white_ref[...] = white
    turned[...] = jnp.transpose(white)
    loads[3].wait()
    sk = split(sketch_ref[...], 2)
    y = dot(white, sk[0], 1, 0) + dot(white, sk[1], 1, 0)
    width = y.shape[1]

    pl.semaphore_wait(barrier, planes + bins + 1)
    first = [remote(send1.at[k], recv1.at[k], 0, k, sibling) for k in range(bins)]
    second = [
        k and remote(send2.at[k], recv2.at[k], 1, k, other(k))
        for k in range(bins)
    ]
    across = [
        k and remote(sendy.at[k], recvy.at[k], 4, k, other(k))
        for k in range(bins)
    ]

    def spread(k):
        return remote(sendv.at[fellow(k) >> 1], recvv.at[k], 2, k, (bin_at, fellow(k)))

    def third(k):
        return remote(send3.at[fellow(k) >> 1], recv3.at[k], 3, k, (bin_at, fellow(k)))

    def fourth(k):
        mine = full.at[core, place]
        return remote(mine, mine, 5, k, (bin_at, fellow(k)))

    def hand(k):
        mine = full.at[core, (place - k) & (planes - 1)]
        return remote(mine, mine, 6, k, sibling)

    def form(k):
        pb = dot(turned[...], jnp.where(bin_col == float(k), y, 0.0).astype(bf16), 1, 0)
        halves[k, 0] = pb[:half]
        halves[k, 1] = pb[half:]
        send1[k] = halves[k, 1 - core].astype(bf16)
        first[k].start()

    def join(k):
        first[k].wait_recv()
        both = (halves[k, core] + recv1[k].astype(f32)).reshape(planes, 2, part, width)
        if k:
            send2[k] = both[:, 0].astype(bf16)
            second[k].start()
        else:
            total[...] = both[:, 0]
        sendv[:, k] = both[:, 1].astype(bf16)

    form(2)
    form(1)
    loads[0].wait()
    xrows = x_ref.shape[1] // LANES
    for d in range(2):
        for i in range(xrows):
            xe[pl.ds(d * (xrows + lead) + lead + i, 1), :] = x_ref[
                d : d + 1, i * LANES : (i + 1) * LANES
            ]
    edges = [
        remote(
            xe.at[pl.ds(d * (xrows + lead) + xrows, lead), :], edge.at[d], 4, bins + d, following
        )
        for d in range(2)
    ]
    for e in edges:
        e.start()
    join(2)
    form(3)
    join(1)
    form(0)
    join(3)
    join(0)

    @pl.loop(1, planes, unroll=True)
    def _(k):
        spread(k).start()

    for d in range(2):
        edges[d].wait_recv()
        xe[pl.ds(d * (xrows + lead), lead), :] = jnp.where(at > 0, edge[d], 0.0)
    decimate(rvs, xe[...])
    for entry in plan[:1]:
        build_strip(entry, rvs[entry[0]], strip)

    for k in range(1, bins):
        second[k].wait_recv()
        total[...] = total[...] + recv2[k].astype(f32)
    send3[...] = total[...].astype(bf16)

    @pl.loop(1, planes, unroll=True)
    def _(k):
        third(k).start()

    @pl.loop(1, planes, unroll=True)
    def _(k):
        spread(k).wait_recv()

    acc = sendv[place].astype(f32)
    for k in range(1, planes):
        acc = acc + recvv[k].astype(f32)
    for k in range(1, bins):
        sendy[k] = acc[k].astype(bf16)
        across[k].start()

    for entry in plan[1:2]:
        build_strip(entry, rvs[entry[0]], strip)

    @pl.loop(1, planes, unroll=True)
    def _(k):
        third(k).wait_recv()

    one = total[place]
    for k in range(1, planes):
        one = one + recv3[k].astype(f32)
    two = acc[0]
    for k in range(1, bins):
        across[k].wait_recv()
        two = two + recvy[k].astype(f32)
    full[core, place] = jnp.concatenate([one, two], axis=0)
    hand(0).start()

    @pl.loop(1, planes, unroll=True)
    def _(k):
        fourth(k).start()

    for entry in plan[2:]:
        build_strip(entry, rvs[entry[0]], strip)

    @pl.loop(1, planes, unroll=True)
    def _(k):
        fourth(k).wait_recv()
        hand(k).start()

    for d in range(2):
        edges[d].wait_send()
    for k in range(bins):
        first[k].wait_send()
    for k in range(1, bins):
        second[k].wait_send()
        across[k].wait_send()

    @pl.loop(1, planes, unroll=True)
    def _(k):
        spread(k).wait_send()
        third(k).wait_send()
        fourth(k).wait_send()

    @pl.loop(0, planes, unroll=True)
    def _(k):
        hand(k).wait()

    product_ref[...] = full[...].reshape(length, width)


def products(bins, group_size, lead, plan, held, templates, owner, rate, gains, sketch, strain):
    rows, length = templates.shape
    width = sketch.shape[1]
    levels = gains.shape[0]
    planes = group_size // 2
    half, part = length // 2, length // group_size // 2
    hbm = lambda: pl.BlockSpec(memory_space=pltpu.HBM)
    xrows = strain.shape[1] // LANES + lead
    vm = lambda: pl.BlockSpec(memory_space=pltpu.VMEM)
    far = lambda a: pltpu.with_memory_space_constraint(a, pltpu.HBM)
    return pl.pallas_call(
        functools.partial(product_kernel, bins, group_size, planes, lead, plan, levels),
        out_shape=[
            jax.ShapeDtypeStruct((rows, length), bf16),
            jax.ShapeDtypeStruct((length, width), f32),
            jax.ShapeDtypeStruct((LANES, held * LANES), bf16),
            jax.ShapeDtypeStruct((1, rows), jnp.int32),
        ],
        in_specs=[hbm() for _ in range(6)],
        out_specs=[vm() for _ in range(4)],
        scratch_shapes=[
            pltpu.VMEM(templates.shape, bf16),
            pltpu.VMEM(owner.shape, jnp.int32),
            pltpu.VMEM(rate.shape, jnp.int32),
            pltpu.VMEM(gains.shape, f32),
            pltpu.VMEM(sketch.shape, f32),
            pltpu.VMEM(strain.shape, f32),
            pltpu.VMEM((length, rows), bf16),
            pltpu.VMEM((bins, 2, half, width), f32),
            pltpu.VMEM((bins, half, width), bf16),
            pltpu.VMEM((bins, half, width), bf16),
            pltpu.VMEM((bins, planes, part, width), bf16),
            pltpu.VMEM((bins, planes, part, width), bf16),
            pltpu.VMEM((planes, bins, part, width), bf16),
            pltpu.VMEM((planes, bins, part, width), bf16),
            pltpu.VMEM((planes, part, width), f32),
            pltpu.VMEM((planes, part, width), bf16),
            pltpu.VMEM((planes, part, width), bf16),
            pltpu.VMEM((bins, part, width), bf16),
            pltpu.VMEM((bins, part, width), bf16),
            pltpu.VMEM((2, planes, 2 * part, width), f32),
            pltpu.VMEM((2, lead, LANES), f32),
            pltpu.VMEM((2 * xrows, LANES), f32),
        ]
        + [pltpu.VMEM((2 * xrows >> r, LANES), f32) for r in range(levels)]
        + [pltpu.SemaphoreType.DMA((6,)), pltpu.SemaphoreType.DMA((7, 2, planes))],
        compiler_params=pltpu.CompilerParams(
            vmem_limit_bytes=30 << 20, collective_id=0, has_side_effects=True
        ),
        name="products",
    )(far(templates), far(owner), far(rate), far(gains), far(sketch), far(strain))


def eliminate(D, nb):
    w, groups = 8, nb // 8
    ri = lax.broadcasted_iota(jnp.int32, (nb, nb), 0)
    ci = lax.broadcasted_iota(jnp.int32, (nb, nb), 1)
    eye = jnp.where(ri == ci, 1.0, 0.0).astype(f32)
    left = [D[8 * k : 8 * k + 8, :] for k in range(groups)]
    right = [eye[8 * k : 8 * k + 8, :] for k in range(groups)]
    sub = lax.broadcasted_iota(jnp.int32, (8, nb), 0)
    spread = lambda x: jnp.broadcast_to(x, (8, nb))
    for g in range(groups):
        j = g * w
        a = [spread(left[g][s : s + 1, :]) for s in range(w)]
        b = [spread(right[g][s : s + 1, :]) for s in range(w)]
        S = [
            [spread(a[s][:, j + t : j + t + 1]) if t >= s else None for t in range(w)]
            for s in range(w)
        ]
        inv = []
        for s in range(w):
            iv = 1.0 / S[s][s]
            inv.append(iv)
            for t in range(s + 1, w):
                f = S[s][t] * iv
                for u in range(t, w):
                    S[t][u] = S[t][u] - f * S[s][u]
                a[t] = a[t] - f * a[s]
                b[t] = b[t] - f * b[s]
        for k in range(g + 1, groups):
            c = [spread(left[k][:, j + s : j + s + 1]) for s in range(w)]
            lk, rk = left[k], right[k]
            for s in range(w):
                m = c[s] * inv[s]
                lk = lk - m * a[s]
                rk = rk - m * b[s]
                for t in range(s + 1, w):
                    c[t] = c[t] - m * S[s][t]
            left[k], right[k] = lk, rk
        l_own, r_own = a[0], b[0]
        for s in range(1, w):
            l_own = jnp.where(sub == s, a[s], l_own)
            r_own = jnp.where(sub == s, b[s], r_own)
        left[g], right[g] = l_own, r_own
    diag = jnp.where(ri == ci, jnp.concatenate(left, axis=0), 0.0)
    d_col = jnp.sum(diag, axis=1, keepdims=True)
    d_row = jnp.sum(diag, axis=0, keepdims=True)
    return jnp.concatenate(right, axis=0) * lax.rsqrt(d_col), d_row * lax.rsqrt(d_row)


def strip_plan(tiles, length, levels, lead):
    plan, base = [], 0
    for r in range(levels):
        blocks = max(1, (length >> r) // LANES)
        rows = (tiles + lead) >> r
        held = (tiles >> r) + blocks - 1
        chunk = next(m for m in (17, 16, 8, 4, 2, 1) if held % m == 0 or (m == 17 and held > 17 and held % 17 >= 15))
        for d in range(2):
            plan.append((r, d, tiles >> r, blocks, rows, chunk, -(-held // chunk), base))
            base += -(-held // chunk) * chunk
    return plan, base


def decimate(rvs, x):
    n = LANES
    ri = lax.broadcasted_iota(jnp.int32, (n, n), 0)
    ci = lax.broadcasted_iota(jnp.int32, (n, n), 1)
    flip = jnp.where(ri + ci == n - 1, 1.0, 0.0).astype(f32)
    first = jnp.where(ri // 2 == ci, 1.0, 0.0).astype(f32)
    second = jnp.where(ri // 2 == ci - n // 2, 1.0, 0.0).astype(f32)
    rvs[0][...] = dot(x, flip, 1, 0, highest)
    for r in range(1, len(rvs)):
        count = rvs[r].shape[0]
        later = rvs[r - 1][pl.ds(1, count, stride=2), :]
        earlier = rvs[r - 1][pl.ds(0, count, stride=2), :]
        rvs[r][...] = (
            dot(later, first, 1, 0, highest) + dot(earlier, second, 1, 0, highest)
        ) * inv_root_two


def build_strip(entry, rv, strip):
    r, d, tiles, blocks, rows, chunk, count, base = entry
    n = LANES
    wide = chunk + 1
    span = (wide + 1) * n

    def step(i, carry):
        q = d * rows + rows - 1 - i * chunk
        z = jnp.concatenate(
            [rv[pl.ds(jnp.maximum(q - j, 0), 1), :] for j in range(wide + 1)], axis=1
        ).astype(bf16).astype(f32)
        z = jnp.broadcast_to(z, (16, span))
        z = pltpu.roll(z, span - 15, 1, stride=1, stride_axis=0)[:, : wide * n]
        at = pl.ds(pl.multiple_of((base + i * chunk) * n, n), chunk * n)
        for g in range(n // 16):
            k = n - 16 - 16 * g
            t = pltpu.roll(z, wide * n - k, 1) if k else z
            strip[16 * g : 16 * g + 16, at] = t[:, : chunk * n].astype(bf16)
        return carry

    lax.fori_loop(0, count, step, 0)


def filter_level(entry, strip, weight, group, emit):
    r, d, tiles, blocks, rows, chunk, count, base = entry
    n = LANES
    group = min(group, tiles)
    span = group * n

    def tile(s, carry):
        parts = []
        for t in range(group):
            p = base + tiles - 1 - (s * group + t)
            parts.append(strip[:, pl.ds(pl.multiple_of(p * n, n), blocks * n)])
        at = pl.ds(pl.multiple_of(s * span, span), span)
        emit(at, dot(jnp.concatenate(parts, axis=0), weight, 1, 0).astype(bf16))
        return carry

    lax.fori_loop(0, tiles // group, tile, 0)


def finish_kernel(
    bins, scale, plan, levels, p_ref, white_ref, bin_ref, strip, basis_ref, spec_ref, mix_ref, *rest
):
    small, (A, bases, bwide, sems) = rest[: levels - 1], rest[levels - 1 :]
    length, width = p_ref.shape
    nb = width // 2
    bin_at, at = lax.axis_index("bin"), lax.axis_index("grp")
    mesh_id = pl.DeviceIdType.MESH

    def other(k):
        return ((bin_at + k) & (bins - 1), at)

    barrier = pltpu.get_barrier_semaphore()
    for k in range(1, bins):
        pl.semaphore_signal(barrier, inc=1, device_id=other(k), device_id_type=mesh_id)
    sends = [
        [
            pltpu.make_async_remote_copy(
                src_ref=bases.at[0, h], dst_ref=bases.at[bins - k, h],
                send_sem=sems.at[0, h, k], recv_sem=sems.at[1, h, k],
                device_id=other(k), device_id_type=mesh_id,
            )
            for k in range(1, bins)
        ]
        for h in range(2)
    ]
    p0 = p_ref[:, :nb]
    A[...] = dot(p_ref[...], p_ref[...], 0, 0, highest)
    x0, d0 = eliminate(A[:nb, :nb], nb)
    q0 = dot(p0, x0, 1, 1, highest)
    basis_ref[:, :nb] = q0.astype(bf16)
    bases[0, 0] = q0.astype(bf16)
    pl.semaphore_wait(barrier, bins - 1)
    for send in sends[0]:
        send.start()
    r01 = dot(x0, A[:nb, nb:], 1, 0, highest)
    left = p_ref[:, nb:] - dot(q0, r01, 1, 0, highest)
    x1, d1 = eliminate(A[nb:, nb:] - dot(r01, r01, 0, 0, highest), nb)
    q1 = dot(left, x1, 1, 1, highest)
    basis_ref[:, nb:] = q1.astype(bf16)
    bases[0, 1] = q1.astype(bf16)
    for send in sends[1]:
        send.start()
    spec_ref[...] = jnp.concatenate([d0, d1], axis=1) * scale
    n = LANES
    for h in range(bwide.shape[0]):
        bwide[h] = basis_ref[:, h * n : (h + 1) * n].astype(f32)
    for entry in plan[2:]:
        r, d = entry[:2]
        taps = length >> r
        weight = jnp.concatenate(
            [bwide[h, pl.ds(0, taps, stride=1 << r), :] for h in range(bwide.shape[0])], axis=1
        )
        if taps < n:
            weight = jnp.concatenate([weight, jnp.zeros((n - taps, width), f32)], axis=0)

        def emit(where, value, r=r, d=d):
            small[r - 1][d, where, :] = value

        filter_level(entry, strip, weight.astype(bf16), 16, emit)
    white = white_ref[...]
    rows = white.shape[0]
    bin_col = jnp.transpose(jnp.broadcast_to(bin_ref[...], (8, rows)).astype(f32))[:, 0:1]
    acc = dot(white, basis_ref[...], 1, 0)
    for h in range(2):
        for send in sends[h]:
            send.wait_recv()
    for k in range(1, bins):
        theirs = jnp.concatenate([bases[k, 0], bases[k, 1]], axis=1)
        acc = jnp.where(bin_col == float(k), dot(white, theirs, 1, 0), acc)
    mix_ref[...] = acc.astype(bf16)
    for h in range(2):
        for send in sends[h]:
            send.wait_send()


def finish(bins, scale, plan, levels, product, white, relative, strip):
    length, width = product.shape
    rows = white.shape[0]
    samples = plan[0][2] * LANES
    vm = lambda: pl.BlockSpec(memory_space=pltpu.VMEM)
    return pl.pallas_call(
        functools.partial(finish_kernel, bins, scale, plan, levels),
        out_shape=[
            jax.ShapeDtypeStruct((length, width), bf16),
            jax.ShapeDtypeStruct((1, width), f32),
            jax.ShapeDtypeStruct((rows, width), bf16),
        ]
        + [jax.ShapeDtypeStruct((2, samples >> r, width), bf16) for r in range(1, levels)],
        in_specs=[vm() for _ in range(4)],
        out_specs=[vm() for _ in range(levels + 2)],
        scratch_shapes=[
            pltpu.VMEM((width, width), f32),
            pltpu.VMEM((bins, 2, length, width // 2), bf16),
            pltpu.VMEM((width // LANES, length, LANES), f32),
            pltpu.SemaphoreType.DMA((2, 2, bins)),
        ],
        compiler_params=pltpu.CompilerParams(
            vmem_limit_bytes=24 << 20, collective_id=1, has_side_effects=True
        ),
        name="finish",
    )(product, white, relative, strip)


def output_kernel(plan, levels, strip, basis_ref, spec_ref, mix_ref, *rest):
    small, outs, held, sems = (
        rest[: levels - 1], rest[levels - 1 : 2 * levels + 1], rest[-2], rest[-1]
    )
    mix_out, spec_out, filtered = outs[0], outs[1], outs[2:]
    stores = [
        pltpu.make_async_copy(src, dst, sems.at[1 + i])
        for i, (src, dst) in enumerate(
            [(small[r - 1], filtered[r].at[0]) for r in range(1, levels)]
            + [(mix_ref, mix_out), (spec_ref, spec_out)]
        )
    ]
    for store in stores:
        store.start()
    weight = basis_ref[...]
    for entry in plan[:2]:
        d = entry[1]

        def emit(where, value, d=d):
            held[d, where, :] = value
            pltpu.make_async_copy(
                held.at[d, where, :], filtered[0].at[0, d, where, :], sems.at[0]
            ).start()

        filter_level(entry, strip, weight, 32, emit)
    pltpu.make_async_copy(held, filtered[0].at[0], sems.at[0]).wait()
    for store in stores:
        store.wait()


def output(plan, levels, strip, basis, spectrum, mixed, small):
    width = basis.shape[1]
    samples = plan[0][2] * LANES
    vm = lambda: pl.BlockSpec(memory_space=pltpu.VMEM)
    return pl.pallas_call(
        functools.partial(output_kernel, plan, levels),
        out_shape=[
            jax.ShapeDtypeStruct(mixed.shape, bf16),
            jax.ShapeDtypeStruct(spectrum.shape, f32),
        ]
        + [jax.ShapeDtypeStruct((1, 2, samples >> r, width), bf16) for r in range(levels)],
        in_specs=[vm() for _ in range(levels + 3)],
        out_specs=[pl.BlockSpec(memory_space=pl.ANY)] * (levels + 2),
        scratch_shapes=[
            pltpu.VMEM((2, samples, width), bf16),
            pltpu.SemaphoreType.DMA((levels + 2,)),
        ],
        compiler_params=pltpu.CompilerParams(vmem_limit_bytes=24 << 20),
        name="output",
    )(strip, basis, spectrum, mixed, *small)


def local(bins, group_size, templates, owner_device, rate_code, rate_gains, sketch, strain):
    rows, length = templates.shape
    levels = rate_gains.shape[0]
    lead = 16
    scale = 1.0 / (rows * group_size * math.sqrt(length))
    plan, held = strip_plan(strain.shape[1] // LANES, length, levels, lead)
    white, product, strip, relative = products(
        bins, group_size, lead, plan, held, templates, owner_device.reshape(1, rows),
        rate_code.reshape(1, rows), rate_gains, sketch, strain,
    )
    basis, spectrum, mixed, *small = finish(
        bins, scale, plan, levels, product, white, relative, strip
    )
    return tuple(output(plan, levels, strip, basis, spectrum, mixed, small))


def solution(mesh):
    return jax.shard_map(
        functools.partial(local, mesh.shape["bin"], mesh.shape["grp"]),
        mesh=mesh,
        in_specs=(
            P(("bin", "grp"), None),
            P(("bin", "grp"), None),
            P(("bin", "grp")),
            P(),
            P(),
            P(None, "grp"),
        ),
        out_specs=(P(("bin", "grp"), None), P("bin", None)) + (P("bin", None, "grp", None),) * 5,
        check_vma=False,
    )
```

time: 64.3 us -> 65.3 us (1.016)
  Pallas kernels: 58.2 us -> 64.3 us
  starting transfers between devices: 3.07 us -> 0 us
  waiting for transfers between devices: 2.23 us -> 0 us
    pallas_call x3 -> x2, Pallas kernels: 23.8 us -> 31.7 us  [the longest x1 25.2 us: finish(): pl.pallas_call(functools.partial(finish_kernel, bins, scale, plan, levels...]
    ppermute x3 -> x0, starting transfers between devices: 3.07 us -> none  [local(): lax.ppermute(basis, 'bin', [(i, (i - k) % bins) for i in range(bins)])]
    ppermute x3 -> x0, waiting for transfers between devices: 2.23 us -> none  [local(): lax.ppermute(basis, 'bin', [(i, (i - k) % bins) for i in range(bins)])]
    pallas_call x1, Pallas kernels: 34.4 us -> 32.7 us  [products(): pl.pallas_call(functools.partial(product_kernel, bins, group_size, planes...]
  transfers between devices with their start and end apart: 3 -> 0, of which waited for: 2 -> 0; matrix products, arithmetic and copies ran while one was open for 0% -> 0% of each run, Pallas kernels for 15% -> 0%
where the time goes in v5:
time: 65.3 us; the launch traced here: 65.2 us
  Pallas kernels  64.3 us (98%)
  between operations  0.83 us (1%)
    pallas_call x1, Pallas kernels, products(): pl.pallas_call(functools.partial(product_kernel, bins, group_size, planes...  32.7 us
    pallas_call x1, Pallas kernels, finish(): pl.pallas_call(functools.partial(finish_kernel, bins, scale, plan, levels...  25.2 us
    pallas_call x1, Pallas kernels, output(): pl.pallas_call(functools.partial(output_kernel, plan, levels), out_shape=...  6.44 us

profile of v5, /device:TPU:1, one launch (start us, length us, event | category | flops | bytes accessed | tf_op | source)
XLA Modules:
  0.0 65.2 jit_solution(15014210980177643483)
XLA Ops:
  0.6 32.7 %products.1 = (bf16[1024,512]{1,0:T(8,128)(2,1)S(1)}, f32[512,256]{1,0:T(8,128)S(1)}, bf16[128,33280]{1,0:T(8,128)(2,1)S(1)}, s32[1,1024]{1,0:T(1,128)S(1)}) custom-call(bf16[1024,512]{1,0:T(8,128)(2,1)} %t_hbm.1, s32[1,1024]{1,0:T(1,128)} %bitcast.2, s32[1,1024]{1,0:T(1,128)} %bitcast.3, f32[5,512]{1,0:T(8,128)} %gains_hbm.1, f32[512,256]{1,0:T(8,128)} %sketch_hbm.1, ...), custom_call_target="tpu_custom_call" | custom-call | tf_op jit(solution)/shard_map/products/pallas_call | solution.py:270
  33.3 25.2 %finish.1 = (bf16[512,256]{1,0:T(8,128)(2,1)S(1)}, f32[1,256]{1,0:T(1,128)S(1)}, bf16[1024,256]{1,0:T(8,128)(2,1)S(1)}, bf16[2,4096,256]{2,1,0:T(8,128)(2,1)S(1)...) custom-call(f32[512,256]{1,0:T(8,128)S(1)} %get-tuple-element.19.p_ref, ...), custom_call_target="tpu_custom_call" | custom-call | tf_op jit(solution)/shard_map/finish/pallas_call | solution.py:513
  58.5 6.4 %output.1 = (bf16[1024,256]{1,0:T(8,128)(2,1)}, f32[1,256]{1,0:T(1,128)}, bf16[1,2,8192,256]{3,2,1,0:T(8,128)(2,1)}, bf16[1,2,4096,256]{3,2,1,0:T(8,128)(2,1)}, ...) custom-call(bf16[128,33280]{1,0:T(8,128)(2,1)S(1)} %get-tuple-element.18.strip, ...), custom_call_target="tpu_custom_call" | custom-call | tf_op jit(solution)/shard_map/output/pallas_call | solution.py:570

commit v6 on v5

--- a/solution.py
+++ b/solution.py
@@ -18,6 +18,12 @@
     return lax.dot_general(
         a, b, (((ca,), (cb,)), ((), ())), precision=precision, preferred_element_type=f32
     )
+
+
+def at_once(start):
+    @pl.when(lax.axis_index("grp") >= 0)
+    def _():
+        start()
 
 
 def split(x, parts):
@@ -140,14 +146,14 @@
         halves[k, 0] = pb[:half]
         halves[k, 1] = pb[half:]
         send1[k] = halves[k, 1 - core].astype(bf16)
-        first[k].start()
+        at_once(lambda: first[k].start())
 
     def join(k):
         first[k].wait_recv()
         both = (halves[k, core] + recv1[k].astype(f32)).reshape(planes, 2, part, width)
         if k:
             send2[k] = both[:, 0].astype(bf16)
-            second[k].start()
+            at_once(lambda: second[k].start())
         else:
             total[...] = both[:, 0]
         sendv[:, k] = both[:, 1].astype(bf16)
@@ -167,8 +173,7 @@
         )
         for d in range(2)
     ]
-    for e in edges:
-        e.start()
+    at_once(lambda: [e.start() for e in edges])
     join(2)
     form(3)
     join(1)
@@ -205,7 +210,7 @@
         acc = acc + recvv[k].astype(f32)
     for k in range(1, bins):
         sendy[k] = acc[k].astype(bf16)
-        across[k].start()
+        at_once(lambda: across[k].start())
 
     for entry in plan[1:2]:
         build_strip(entry, rvs[entry[0]], strip)
@@ -462,16 +467,14 @@
     basis_ref[:, :nb] = q0.astype(bf16)
     bases[0, 0] = q0.astype(bf16)
     pl.semaphore_wait(barrier, bins - 1)
-    for send in sends[0]:
-        send.start()
+    at_once(lambda: [send.start() for send in sends[0]])
     r01 = dot(x0, A[:nb, nb:], 1, 0, highest)
     left = p_ref[:, nb:] - dot(q0, r01, 1, 0, highest)
     x1, d1 = eliminate(A[nb:, nb:] - dot(r01, r01, 0, 0, highest), nb)
     q1 = dot(left, x1, 1, 1, highest)
     basis_ref[:, nb:] = q1.astype(bf16)
     bases[0, 1] = q1.astype(bf16)
-    for send in sends[1]:
-        send.start()
+    at_once(lambda: [send.start() for send in sends[1]])
     spec_ref[...] = jnp.concatenate([d0, d1], axis=1) * scale
     n = LANES
     for h in range(bwide.shape[0]):

time: 65.3 us -> 60.7 us (0.930)
  Pallas kernels: 64.3 us -> 59.8 us
    pallas_call x1, Pallas kernels: 25.2 us -> 20.5 us  [finish(): pl.pallas_call(functools.partial(finish_kernel, bins, scale, plan, levels...]
where the time goes in v6:
time: 60.7 us; the launch traced here: 60.6 us
  Pallas kernels  59.8 us (99%)
  between operations  0.83 us (1%)
    pallas_call x1, Pallas kernels, products(): pl.pallas_call(functools.partial(product_kernel, bins, group_size, planes...  32.8 us
    pallas_call x1, Pallas kernels, finish(): pl.pallas_call(functools.partial(finish_kernel, bins, scale, plan, levels...  20.5 us
    pallas_call x1, Pallas kernels, output(): pl.pallas_call(functools.partial(output_kernel, plan, levels), out_shape=...  6.45 us

profile of v6, /device:TPU:1, one launch (start us, length us, event | category | flops | bytes accessed | tf_op | source)
XLA Modules:
  0.0 60.6 jit_solution(2148469376915126511)
XLA Ops:
  0.6 32.8 %products.1 = (bf16[1024,512]{1,0:T(8,128)(2,1)S(1)}, f32[512,256]{1,0:T(8,128)S(1)}, bf16[128,33280]{1,0:T(8,128)(2,1)S(1)}, s32[1,1024]{1,0:T(1,128)S(1)}) custom-call(bf16[1024,512]{1,0:T(8,128)(2,1)} %t_hbm.1, s32[1,1024]{1,0:T(1,128)} %bitcast.2, s32[1,1024]{1,0:T(1,128)} %bitcast.3, f32[5,512]{1,0:T(8,128)} %gains_hbm.1, f32[512,256]{1,0:T(8,128)} %sketch_hbm.1, ...), custom_call_target="tpu_custom_call" | custom-call | tf_op jit(solution)/shard_map/products/pallas_call | solution.py:275
  33.5 20.5 %finish.1 = (bf16[512,256]{1,0:T(8,128)(2,1)S(1)}, f32[1,256]{1,0:T(1,128)S(1)}, bf16[1024,256]{1,0:T(8,128)(2,1)S(1)}, bf16[2,4096,256]{2,1,0:T(8,128)(2,1)S(1)...) custom-call(f32[512,256]{1,0:T(8,128)S(1)} %get-tuple-element.19.p_ref, ...), custom_call_target="tpu_custom_call" | custom-call | tf_op jit(solution)/shard_map/finish/pallas_call | solution.py:516
  54.0 6.5 %output.1 = (bf16[1024,256]{1,0:T(8,128)(2,1)}, f32[1,256]{1,0:T(1,128)}, bf16[1,2,8192,256]{3,2,1,0:T(8,128)(2,1)}, bf16[1,2,4096,256]{3,2,1,0:T(8,128)(2,1)}, ...) custom-call(bf16[128,33280]{1,0:T(8,128)(2,1)S(1)} %get-tuple-element.18.strip, ...), custom_call_target="tpu_custom_call" | custom-call | tf_op jit(solution)/shard_map/output/pallas_call | solution.py:573

commit v7 on v6

--- a/solution.py
+++ b/solution.py
@@ -446,18 +446,31 @@
     def other(k):
         return ((bin_at + k) & (bins - 1), at)
 
+    core = at & 1
+    sibling = (bin_at, at + 1 - 2 * core)
     barrier = pltpu.get_barrier_semaphore()
-    for k in range(1, bins):
-        pl.semaphore_signal(barrier, inc=1, device_id=other(k), device_id_type=mesh_id)
+    for peer in [other(k) for k in range(1, bins)] + [sibling]:
+        pl.semaphore_signal(barrier, inc=1, device_id=peer, device_id_type=mesh_id)
+
+    def remote(src, dst, group, h, k, device):
+        return pltpu.make_async_remote_copy(
+            src_ref=src, dst_ref=dst, send_sem=sems.at[group, 0, h, k],
+            recv_sem=sems.at[group, 1, h, k], device_id=device, device_id_type=mesh_id,
+        )
+
+    farthest_first = sorted(range(1, bins), key=lambda k: -min(k, bins - k))
     sends = [
-        [
-            pltpu.make_async_remote_copy(
-                src_ref=bases.at[0, h], dst_ref=bases.at[bins - k, h],
-                send_sem=sems.at[0, h, k], recv_sem=sems.at[1, h, k],
-                device_id=other(k), device_id_type=mesh_id,
-            )
-            for k in range(1, bins)
-        ]
+        {
+            k: remote(bases.at[0, h, core], bases.at[bins - k, h, core], 0, h, k, other(k))
+            for k in farthest_first
+        }
+        for h in range(2)
+    ]
+    hands = [
+        {
+            k: remote(bases.at[bins - k, h, core], bases.at[bins - k, h, core], 1, h, k, sibling)
+            for k in farthest_first
+        }
         for h in range(2)
     ]
     p0 = p_ref[:, :nb]
@@ -465,16 +478,19 @@
     x0, d0 = eliminate(A[:nb, :nb], nb)
     q0 = dot(p0, x0, 1, 1, highest)
     basis_ref[:, :nb] = q0.astype(bf16)
-    bases[0, 0] = q0.astype(bf16)
-    pl.semaphore_wait(barrier, bins - 1)
-    at_once(lambda: [send.start() for send in sends[0]])
+    bases[0, 0] = q0.astype(bf16).reshape(2, length // 2, nb)
+    pl.semaphore_wait(barrier, bins)
+    at_once(lambda: [send.start() for send in sends[0].values()])
     r01 = dot(x0, A[:nb, nb:], 1, 0, highest)
     left = p_ref[:, nb:] - dot(q0, r01, 1, 0, highest)
     x1, d1 = eliminate(A[nb:, nb:] - dot(r01, r01, 0, 0, highest), nb)
     q1 = dot(left, x1, 1, 1, highest)
     basis_ref[:, nb:] = q1.astype(bf16)
-    bases[0, 1] = q1.astype(bf16)
-    at_once(lambda: [send.start() for send in sends[1]])
+    bases[0, 1] = q1.astype(bf16).reshape(2, length // 2, nb)
+    at_once(lambda: [send.start() for send in sends[1].values()])
+    for k in farthest_first:
+        sends[0][k].wait_recv()
+    at_once(lambda: [hand.start() for hand in hands[0].values()])
     spec_ref[...] = jnp.concatenate([d0, d1], axis=1) * scale
     n = LANES
     for h in range(bwide.shape[0]):
@@ -496,16 +512,20 @@
     rows = white.shape[0]
     bin_col = jnp.transpose(jnp.broadcast_to(bin_ref[...], (8, rows)).astype(f32))[:, 0:1]
     acc = dot(white, basis_ref[...], 1, 0)
-    for h in range(2):
-        for send in sends[h]:
-            send.wait_recv()
-    for k in range(1, bins):
-        theirs = jnp.concatenate([bases[k, 0], bases[k, 1]], axis=1)
-        acc = jnp.where(bin_col == float(k), dot(white, theirs, 1, 0), acc)
+    for k in reversed(farthest_first):
+        sends[1][k].wait_recv()
+        at_once(lambda k=k: hands[1][k].start())
+    for k in reversed(farthest_first):
+        for h in range(2):
+            hands[h][k].wait_recv()
+        slot = bins - k
+        theirs = jnp.concatenate([bases[slot, h].reshape(length, nb) for h in range(2)], axis=1)
+        acc = jnp.where(bin_col == float(slot), dot(white, theirs, 1, 0), acc)
     mix_ref[...] = acc.astype(bf16)
     for h in range(2):
-        for send in sends[h]:
-            send.wait_send()
+        for k in farthest_first:
+            sends[h][k].wait_send()
+            hands[h][k].wait_send()
 
 
 def finish(bins, scale, plan, levels, product, white, relative, strip):
@@ -525,9 +545,9 @@
         out_specs=[vm() for _ in range(levels + 2)],
         scratch_shapes=[
             pltpu.VMEM((width, width), f32),
-            pltpu.VMEM((bins, 2, length, width // 2), bf16),
+            pltpu.VMEM((bins, 2, 2, length // 2, width // 2), bf16),
             pltpu.VMEM((width // LANES, length, LANES), f32),
-            pltpu.SemaphoreType.DMA((2, 2, bins)),
+            pltpu.SemaphoreType.DMA((2, 2, 2, bins)),
         ],
         compiler_params=pltpu.CompilerParams(
             vmem_limit_bytes=24 << 20, collective_id=1, has_side_effects=True

time: 60.7 us -> 59.9 us (0.987)
  Pallas kernels: 59.8 us -> 58.9 us
    pallas_call x1, Pallas kernels: 20.5 us -> 19.6 us  [finish(): pl.pallas_call(functools.partial(finish_kernel, bins, scale, plan, levels...]
where the time goes in v7:
time: 59.9 us; the launch traced here: 59.8 us
  Pallas kernels  58.9 us (98%)
  between operations  0.83 us (1%)
    pallas_call x1, Pallas kernels, products(): pl.pallas_call(functools.partial(product_kernel, bins, group_size, planes...  32.8 us
    pallas_call x1, Pallas kernels, finish(): pl.pallas_call(functools.partial(finish_kernel, bins, scale, plan, levels...  19.6 us
    pallas_call x1, Pallas kernels, output(): pl.pallas_call(functools.partial(output_kernel, plan, levels), out_shape=...  6.46 us

profile of v7, /device:TPU:1, one launch (start us, length us, event | category | flops | bytes accessed | tf_op | source)
XLA Modules:
  0.0 59.8 jit_solution(4270768883317146597)
XLA Ops:
  0.6 32.8 %products.1 = (bf16[1024,512]{1,0:T(8,128)(2,1)S(1)}, f32[512,256]{1,0:T(8,128)S(1)}, bf16[128,33280]{1,0:T(8,128)(2,1)S(1)}, s32[1,1024]{1,0:T(1,128)S(1)}) custom-call(bf16[1024,512]{1,0:T(8,128)(2,1)} %t_hbm.1, s32[1,1024]{1,0:T(1,128)} %bitcast.2, s32[1,1024]{1,0:T(1,128)} %bitcast.3, f32[5,512]{1,0:T(8,128)} %gains_hbm.1, f32[512,256]{1,0:T(8,128)} %sketch_hbm.1, ...), custom_call_target="tpu_custom_call" | custom-call | tf_op jit(solution)/shard_map/products/pallas_call | solution.py:275
  33.5 19.6 %finish.1 = (bf16[512,256]{1,0:T(8,128)(2,1)S(1)}, f32[1,256]{1,0:T(1,128)S(1)}, bf16[1024,256]{1,0:T(8,128)(2,1)S(1)}, bf16[2,4096,256]{2,1,0:T(8,128)(2,1)S(1)...) custom-call(f32[512,256]{1,0:T(8,128)S(1)} %get-tuple-element.19.p_ref, ...), custom_call_target="tpu_custom_call" | custom-call | tf_op jit(solution)/shard_map/finish/pallas_call | solution.py:536
  53.1 6.5 %output.1 = (bf16[1024,256]{1,0:T(8,128)(2,1)}, f32[1,256]{1,0:T(1,128)}, bf16[1,2,8192,256]{3,2,1,0:T(8,128)(2,1)}, bf16[1,2,4096,256]{3,2,1,0:T(8,128)(2,1)}, ...) custom-call(bf16[128,33280]{1,0:T(8,128)(2,1)S(1)} %get-tuple-element.18.strip, ...), custom_call_target="tpu_custom_call" | custom-call | tf_op jit(solution)/shard_map/output/pallas_call | solution.py:593
